TPU v7x, 512 devices: a whole 4x8x8 slice. The times are simulated.
512 devices in a mesh: seq: 64 (over z, y), head: 8 (over x, core).
Axes of the slice: x: 4, y: 8, z: 8, core: 2. Of those that a mesh axis runs over, the one named last changes fastest.
Arguments:
- tokens: bfloat16 [32768, 1024], P('seq'), may hold values from -40 to 40
- w_qkv: bfloat16 [1024, 3072], P(None, 'head'), may hold values from -1 to 1
- w_out: bfloat16 [1024, 1024], P('head'), may hold values from -0.1875 to 0.1875
- offsets: int32 [5, 8], replicated, may hold values from 0 to 15, as said below
Outputs:
- mixed: bfloat16 [32768, 1024], P(('seq', 'head'))
Inputs may be any that keep to these rules, and one draw needn't show every extreme that they name: offsets[b, h] lies in 0 .. 2^b - 1.
All inputs are finite; a program needn't handle non-finite values.
Results may differ from a plain program's by a relative error of at most 0.019.
Values may be sent and summed in bfloat16 or wider, within the bound.
A program may use at most 128 MiB of HBM per device.

v0:
```python
import math

import jax
import jax.numpy as jnp
from jax import lax
from jax.sharding import PartitionSpec as P

HD = 128
NB = 5


def partner(x, axis, stride):
    return lax.ppermute(x, axis, [(i, i ^ 1 << stride) for i in range(lax.axis_size(axis))])


def pick_rows(source_block, offset, stride):
    shaped = source_block.reshape(source_block.shape[0] // stride, stride, source_block.shape[1])
    return lax.dynamic_index_in_dim(shaped, offset, 1, keepdims=False)


def restore(values, offset, stride):
    value_rows = values.shape[0]
    expanded = values[:, None]
    onehot = (jnp.arange(stride, dtype=jnp.int32) == offset).reshape(
        (1, stride) + (1,) * (values.ndim - 1)
    )
    filled = jnp.where(onehot, expanded, jnp.zeros_like(expanded))
    return filled.reshape((value_rows * stride,) + values.shape[1:])


def attend(query, key_values, score_scale):
    head_dim = query.shape[1]
    scores = (
        lax.dot_general(
            query,
            key_values[:, :head_dim],
            (((1,), (1,)), ((), ())),
            preferred_element_type=jnp.float32,
        )
        * score_scale
    )
    row_max = jnp.max(scores, axis=1)
    expo = jnp.exp(scores - row_max[:, None])
    row_sum = jnp.sum(expo, axis=1)
    weighted = jnp.dot(
        expo.astype(jnp.bfloat16), key_values[:, head_dim:], preferred_element_type=jnp.float32
    )
    return (row_max, row_sum, weighted)


def merge_branch(running, row_max, row_sum, weighted, offset, stride):
    max_full = restore(row_max, offset, stride)
    sum_full = restore(row_sum, offset, stride)
    weighted_full = restore(weighted, offset, stride)
    if running is None:
        return (max_full, sum_full, weighted_full)
    run_max, run_sum, summed = running
    selected = jnp.arange(run_max.shape[0], dtype=jnp.int32) % stride == offset
    branch_max = jnp.where(selected, max_full, run_max)
    new_max = jnp.maximum(run_max, branch_max)
    decay_old = jnp.exp(run_max - new_max)
    weight_new = jnp.where(selected, jnp.exp(branch_max - new_max), jnp.zeros_like(new_max))
    run_sum = run_sum * decay_old + weight_new * sum_full
    summed = summed * decay_old[:, None] + weight_new[:, None] * weighted_full
    return (new_max, run_sum, summed)


def spread(buffer, bit_total):
    for bit_index in range(bit_total):
        partner_rows = partner(buffer, "seq", bit_index)
        buffer = jnp.concatenate([buffer, partner_rows], axis=0)
    return buffer


def on_device(tokens, w_qkv, w_out, offsets):
    local_heads = w_qkv.shape[1] // (3 * HD)
    seq_count = lax.axis_size("seq")
    score_scale = 1.0 / math.sqrt(HD)
    projected = jnp.dot(tokens, w_qkv, preferred_element_type=jnp.float32).astype(jnp.bfloat16)
    first_head = lax.axis_index("head") * local_heads
    offset_table = [[offsets[branch, first_head + 0]] for branch in range(NB)]
    queries = projected[:, 0:HD]
    key_values = projected[:, HD : 3 * HD]
    picked = []
    bit_counts = []
    for branch in range(NB):
        stride = 2**branch
        picked.append(pick_rows(key_values, offset_table[branch][0], stride))
        group_size = seq_count * stride // 16
        bit_counts.append(group_size.bit_length() - 1)
    gathered = [spread(picked[branch], bit_counts[branch]) for branch in range(NB)]
    running = None
    for branch in range(NB):
        stride = 2**branch
        offset = offset_table[branch][0]
        query = pick_rows(queries, offset, stride)
        head_pairs = gathered[branch]
        row_max, row_sum, weighted = attend(query, head_pairs, score_scale)
        running = merge_branch(running, row_max, row_sum, weighted, offset, stride)
    run_max, run_sum, summed = running
    outputs = (summed / run_sum[:, None]).astype(jnp.bfloat16)
    return lax.psum_scatter(
        jnp.dot(outputs, w_out, preferred_element_type=jnp.float32).astype(jnp.bfloat16),
        "head",
        scatter_dimension=0,
        tiled=True,
    )


def solution(mesh):
    in_specs = (P("seq", None), P(None, "head"), P("head", None), P())
    out_specs = P(("seq", "head"), None)
    return jax.shard_map(
        on_device, mesh=mesh, in_specs=in_specs, out_specs=out_specs, check_vma=False
    )
```

profile of v0, /device:TPU:1, one launch (start us, length us, event | category | flops | bytes accessed | tf_op | source)
XLA Modules:
  0.0 264.2 jit_solution(299552657682173658)
XLA Ops:
  6.5 1.2 copy-done
  7.8 1.8 convolution_convert_fusion.1
  9.6 4.0 %collective-permute-start = (bf16[512,256]{1,0:T(8,128)(2,1)S(1)}, bf16[512,256]{1,0:T(8,128)(2,1)S(1)}, u32[]{:S(2)}, u32[]{:S(2)}) collective-permute-start(bf16[512,256]{1,0:T(8,128)(2,1)S(1)} %get-tuple-element.25), channel_id=1, source_target_pairs={{0,8},{8,0},{16,24},{24,16},{32,40},{40,32},{48,56},{56,48},{64,72... | collective-permute-start | bytes 786440 | tf_op jit(solution)/shard_map/ppermute | solution.py:13
  13.8 0.7 constant_dynamic-slice_fusion.8
  16.5 1.9 collective-permute-start.2
  21.0 3.4 %collective-permute-start.9 = (bf16[64,256]{1,0:T(8,128)(2,1)S(1)}, bf16[64,256]{1,0:T(8,128)(2,1)S(1)}, u32[]{:S(2)}, u32[]{:S(2)}) collective-permute-start(bf16[64,256]{1,0:T(8,128)(2,1)S(1)} %get-tuple-element.15), channel_id=1, source_target_pairs={{0,8},{8,0},{16,24},{24,16},{32,40},{40,32},{48,56},{56,48},{64,72... | collective-permute-start | bytes 98312 | tf_op jit(solution)/shard_map/ppermute | solution.py:13
  26.9 1.9 collective-permute-start.14
  31.0 3.4 %collective-permute-start.5 = (bf16[128,256]{1,0:T(8,128)(2,1)S(1)}, bf16[128,256]{1,0:T(8,128)(2,1)S(1)}, u32[]{:S(2)}, u32[]{:S(2)}) collective-permute-start(bf16[128,256]{1,0:T(8,128)(2,1)S(1)} %get-tuple-element.19), channel_id=1, source_target_pairs={{0,8},{8,0},{16,24},{24,16},{32,40},{40,32},{48,56},{56,48},{64,72... | collective-permute-start | bytes 196616 | tf_op jit(solution)/shard_map/ppermute | solution.py:13
  34.4 0.7 iota_compare_fusion.2
  35.1 1.1 iota_compare_fusion.3
  38.1 0.6 constant_dynamic-slice_fusion.3
  38.7 0.7 constant_dynamic-slice_fusion.5
  39.5 0.8 constant_dynamic-slice_fusion.7
  40.9 0.7 broadcast_in_dim.335
  42.2 0.7 broadcast_in_dim.321
  43.5 0.7 broadcast_in_dim.314
  44.9 4.2 %collective-permute-start.15 = (bf16[64,256]{1,0:T(8,128)(2,1)S(1)}, bf16[64,256]{1,0:T(8,128)(2,1)S(1)}, u32[]{:S(2)}, u32[]{:S(2)}) collective-permute-start(bf16[64,256]{1,0:T(8,128)(2,1)S(1)} %pad_maximum_fusion.13), channel_id=1, source_target_pairs={{0,16},{8,24},{16,0},{24,8},{32,48},{40,56},{48,32},{56,40},{64,80... | collective-permute-start | bytes 98312 | tf_op jit(solution)/shard_map/ppermute | solution.py:13
  49.7 2.0 collective-permute-start.10
  51.7 0.6 constant_dynamic-update-slice_fusion.8
  52.4 6.6 %collective-permute-start.16 = (bf16[128,256]{1,0:T(8,128)(2,1)S(1)}, bf16[128,256]{1,0:T(8,128)(2,1)S(1)}, u32[]{:S(2)}, u32[]{:S(2)}) collective-permute-start(bf16[128,256]{1,0:T(8,128)(2,1)S(1)} %pad_maximum_fusion.12), channel_id=1, source_target_pairs={{0,32},{8,40},{16,48},{24,56},{32,0},{40,8},{48,16},{56,24},{64,96... | collective-permute-start | bytes 196616 | tf_op jit(solution)/shard_map/ppermute | solution.py:13
  58.9 0.6 constant_dynamic-update-slice_fusion.24
  59.6 2.4 collective-permute-start.6
  62.0 4.4 %collective-permute-start.11 = (bf16[256,256]{1,0:T(8,128)(2,1)S(1)}, bf16[256,256]{1,0:T(8,128)(2,1)S(1)}, u32[]{:S(2)}, u32[]{:S(2)}) collective-permute-start(bf16[256,256]{1,0:T(8,128)(2,1)S(1)} %pad_maximum_fusion.9), channel_id=1, source_target_pairs={{0,32},{8,40},{16,48},{24,56},{32,0},{40,8},{48,16},{56,24},{64,96... | collective-permute-start | bytes 393224 | tf_op jit(solution)/shard_map/ppermute | solution.py:13
  66.5 0.7 constant_dynamic-update-slice_fusion.7
  67.2 4.0 %collective-permute-start.17 = (bf16[256,256]{1,0:T(8,128)(2,1)S(1)}, bf16[256,256]{1,0:T(8,128)(2,1)S(1)}, u32[]{:S(2)}, u32[]{:S(2)}) collective-permute-start(bf16[256,256]{1,0:T(8,128)(2,1)S(1)} %pad_maximum_fusion.10), channel_id=1, source_target_pairs={{0,64},{8,72},{16,80},{24,88},{32,96},{40,104},{48,112},{56,120},{... | collective-permute-start | bytes 393224 | tf_op jit(solution)/shard_map/ppermute | solution.py:13
  71.2 0.7 constant_dynamic-update-slice_fusion.23
  71.9 2.1 collective-permute-start.3
  74.0 6.6 %collective-permute-start.7 = (bf16[512,256]{1,0:T(8,128)(2,1)S(1)}, bf16[512,256]{1,0:T(8,128)(2,1)S(1)}, u32[]{:S(2)}, u32[]{:S(2)}) collective-permute-start(bf16[512,256]{1,0:T(8,128)(2,1)S(1)} %pad_maximum_fusion.6), channel_id=1, source_target_pairs={{0,32},{8,40},{16,48},{24,56},{32,0},{40,8},{48,16},{56,24},{64,96... | collective-permute-start | bytes 786440 | tf_op jit(solution)/shard_map/ppermute | solution.py:13
  80.7 1.9 collective-permute-start.12
  82.6 0.7 constant_dynamic-update-slice_fusion.6
  83.3 0.7 constant_dynamic-update-slice_fusion.22
  84.1 5.8 %collective-permute-start.18 = (bf16[512,256]{1,0:T(8,128)(2,1)S(1)}, bf16[512,256]{1,0:T(8,128)(2,1)S(1)}, u32[]{:S(2)}, u32[]{:S(2)}) collective-permute-start(bf16[512,256]{1,0:T(8,128)(2,1)S(1)} %get-tuple-element.34), channel_id=1, source_target_pairs={{0,128},{8,136},{16,144},{24,152},{32,160},{40,168},{48,176},{56,1... | collective-permute-start | bytes 786440 | tf_op jit(solution)/shard_map/ppermute | solution.py:13
  89.9 2.4 collective-permute-start.1
  92.4 7.3 %collective-permute-done.3 = bf16[512,256]{1,0:T(8,128)(2,1)S(1)} collective-permute-done((bf16[512,256]{1,0:T(8,128)(2,1)S(1)}, bf16[512,256]{1,0:T(8,128)(2,1)S(1)}, u32[]{:S(2)}, u32[]{:S(2)}) %collective-permute-start.3) | collective-permute-done | bytes 262176 | tf_op jit(solution)/shard_map/ppermute | solution.py:13
  99.7 5.8 %collective-permute-start.4 = (bf16[1024,256]{1,0:T(8,128)(2,1)S(1)}, bf16[1024,256]{1,0:T(8,128)(2,1)S(1)}, u32[]{:S(2)}, u32[]{:S(2)}) collective-permute-start(bf16[1024,256]{1,0:T(8,128)(2,1)S(1)} %pad_maximum_fusion.3), channel_id=1, source_target_pairs={{0,32},{8,40},{16,48},{24,56},{32,0},{40,8},{48,16},{56,24},{64,96... | collective-permute-start | bytes 1572872 | tf_op jit(solution)/shard_map/ppermute | solution.py:13
  105.5 0.8 pad_maximum_fusion.4
  106.3 1.9 collective-permute-start.8
  108.3 0.9 constant_dynamic-update-slice_fusion.5
  109.2 3.7 %collective-permute-start.13 = (bf16[1024,256]{1,0:T(8,128)(2,1)}, bf16[1024,256]{1,0:T(8,128)(2,1)}, u32[]{:S(2)}, u32[]{:S(2)}) collective-permute-start(bf16[1024,256]{1,0:T(8,128)(2,1)} %get-tuple-element.26), channel_id=1, source_target_pairs={{0,128},{8,136},{16,144},{24,152},{32,160},{40,168},{48,176},{56,1... | collective-permute-start | bytes 1572872 | tf_op jit(solution)/shard_map/ppermute | solution.py:13
  113.0 0.9 constant_dynamic-update-slice_fusion.21
  113.8 3.8 %collective-permute-start.19 = (bf16[1024,256]{1,0:T(8,128)(2,1)}, bf16[1024,256]{1,0:T(8,128)(2,1)}, u32[]{:S(2)}, u32[]{:S(2)}) collective-permute-start(bf16[1024,256]{1,0:T(8,128)(2,1)} %get-tuple-element.28), channel_id=1, source_target_pairs={{0,256},{8,264},{16,272},{24,280},{32,288},{40,296},{48,304},{56,3... | collective-permute-start | bytes 1572872 | tf_op jit(solution)/shard_map/ppermute | solution.py:13
  117.7 0.8 multiply_reduce_fusion
  118.7 1.9 fusion
  120.7 10.0 %collective-permute-done.4 = bf16[1024,256]{1,0:T(8,128)(2,1)S(1)} collective-permute-done((bf16[1024,256]{1,0:T(8,128)(2,1)S(1)}, bf16[1024,256]{1,0:T(8,128)(2,1)S(1)}, u32[]{:S(2)}, u32[]{:S(2)}) %collective-permute-start.4) | collective-permute-done | bytes 524320 | tf_op jit(solution)/shard_map/ppermute | solution.py:13
  130.8 1.0 copy-done.2
  133.1 0.7 broadcast_in_dim.342
  133.8 1.6 fusion.43
  135.5 1.1 constant_dynamic-update-slice_fusion
  136.6 1.0 copy-done.7
  138.5 0.7 broadcast_in_dim.344
  139.2 1.8 fusion.113
  141.1 2.0 fusion.48
  143.1 2.0 constant_dynamic-update-slice_fusion.10
  145.1 1.5 fusion.122
  146.6 0.7 broadcast_in_dim.330
  147.6 0.7 broadcast_in_dim.346
  148.3 1.9 fusion.53
  150.2 2.9 %collective-permute-done.19 = bf16[1024,256]{1,0:T(8,128)(2,1)} collective-permute-done((bf16[1024,256]{1,0:T(8,128)(2,1)}, bf16[1024,256]{1,0:T(8,128)(2,1)}, u32[]{:S(2)}, u32[]{:S(2)}) %collective-permute-start.19) | collective-permute-done | bytes 524320 | tf_op jit(solution)/shard_map/ppermute | solution.py:13
  153.2 1.1 constant_dynamic-update-slice_fusion.27
  155.4 3.3 %multiply_add_fusion = (f32[512]{0:T(512)S(1)}, f32[512]{0:T(512)S(1)}, f32[512]{0:T(512)S(1)}, f32[512]{0:T(512)S(1)}, f32[512]{0:T(512)S(1)}, /*index=5*/f32[5...) fusion(pred[512]{0:T(512)(128)(4,1)} %broadcast_in_dim.335, f32[512]{0:T(512)S(1)} %broadcast_in_dim.348, ...), kind=kLoop, calls=%fused_computation.155 | loop fusion | flops 34816 | bytes 45073 | tf_op jit(solution)/shard_map/add | solution.py:63
  158.7 0.9 fusion.68
  159.6 0.9 broadcast_in_dim.325
  160.6 4.5 %convolution_convert_fusion = bf16[512,1024]{1,0:T(8,128)(2,1)} fusion(bf16[128,1024]{1,0:T(8,128)(2,1)} %param.6, f32[512,128]{1,0:T(8,128)S(1)} %fusion.68, f32[512,2048]{1,0:T(8,128)} %copy-done.1, f32[512]{0:T(512)} %copy-done.12, bf16[2048,256]{1,0:T(8,128)(2,1)S(1)} %copy-done.4, f32[512,128]{1,0:T(8,128)S(1)} %bitcast.69, ...), kind=kOutput, calls=%fused_computation.14 | convolution fusion | flops 407437312 | bytes 6868481 | tf_op jit(solution)/shard_map/dot_general | solution.py:103
  165.2 92.2 %reduce-scatter.2.cloned.1.call-done = bf16[64,1024]{1,0:T(8,128)(2,1)} async-done(((bf16[512,1024]{1,0:T(8,128)(2,1)}), bf16[64,1024]{1,0:T(8,128)(2,1)}) %reduce-scatter.2.cloned.1.call-update) | async-done | bytes 131088 | tf_op jit(solution)/shard_map/reduce_scatter | solution.py:102
  (114 shorter events, 11.1 us)
Async XLA Ops:
  6.5 1.2 copy-start
  6.5 7.3 %copy-start.17 = (s32[5,8]{1,0:T(8,128)S(1)}, s32[5,8]{1,0:T(8,128)}, u32[]{:S(2)}) copy-start(s32[5,8]{1,0:T(8,128)} %param.7) | copy-start | bytes 484
  6.5 250.8 %reduce-scatter.2.cloned.1.call-start = ((), (), s32[]{:S(2)}) async-start(), calls=%async_computation.1 | async-start | bytes 1179648 | tf_op jit(solution)/shard_map/reduce_scatter | solution.py:102
  9.6 80.2 %collective-permute-start = (bf16[512,256]{1,0:T(8,128)(2,1)S(1)}, bf16[512,256]{1,0:T(8,128)(2,1)S(1)}, u32[]{:S(2)}, u32[]{:S(2)}) collective-permute-start(bf16[512,256]{1,0:T(8,128)(2,1)S(1)} %get-tuple-element.25), channel_id=1, source_target_pairs={{0,8},{8,0},{16,24},{24,16},{32,40},{40,32},{48,56},{56,48},{64,72... | collective-permute-start | bytes 786440 | tf_op jit(solution)/shard_map/ppermute | solution.py:13
  16.5 55.4 %collective-permute-start.2 = (bf16[256,256]{1,0:T(8,128)(2,1)S(1)}, bf16[256,256]{1,0:T(8,128)(2,1)S(1)}, u32[]{:S(2)}, u32[]{:S(2)}) collective-permute-start(bf16[256,256]{1,0:T(8,128)(2,1)S(1)} %bitcast.62), channel_id=1, source_target_pairs={{0,8},{8,0},{16,24},{24,16},{32,40},{40,32},{48,56},{56,48},{64,72... | collective-permute-start | bytes 393224 | tf_op jit(solution)/shard_map/ppermute | solution.py:13
  21.0 28.7 %collective-permute-start.9 = (bf16[64,256]{1,0:T(8,128)(2,1)S(1)}, bf16[64,256]{1,0:T(8,128)(2,1)S(1)}, u32[]{:S(2)}, u32[]{:S(2)}) collective-permute-start(bf16[64,256]{1,0:T(8,128)(2,1)S(1)} %get-tuple-element.15), channel_id=1, source_target_pairs={{0,8},{8,0},{16,24},{24,16},{32,40},{40,32},{48,56},{56,48},{64,72... | collective-permute-start | bytes 98312 | tf_op jit(solution)/shard_map/ppermute | solution.py:13
  26.9 18.0 %collective-permute-start.14 = (bf16[32,256]{1,0:T(8,128)(2,1)S(1)}, bf16[32,256]{1,0:T(8,128)(2,1)S(1)}, u32[]{:S(2)}, u32[]{:S(2)}) collective-permute-start(bf16[32,256]{1,0:T(8,128)(2,1)S(1)} %get-tuple-element.21), channel_id=1, source_target_pairs={{0,8},{8,0},{16,24},{24,16},{32,40},{40,32},{48,56},{56,48},{64,72... | collective-permute-start | bytes 49160 | tf_op jit(solution)/shard_map/ppermute | solution.py:13
  31.0 28.5 %collective-permute-start.5 = (bf16[128,256]{1,0:T(8,128)(2,1)S(1)}, bf16[128,256]{1,0:T(8,128)(2,1)S(1)}, u32[]{:S(2)}, u32[]{:S(2)}) collective-permute-start(bf16[128,256]{1,0:T(8,128)(2,1)S(1)} %get-tuple-element.19), channel_id=1, source_target_pairs={{0,8},{8,0},{16,24},{24,16},{32,40},{40,32},{48,56},{56,48},{64,72... | collective-permute-start | bytes 196616 | tf_op jit(solution)/shard_map/ppermute | solution.py:13
  44.9 7.5 %collective-permute-start.15 = (bf16[64,256]{1,0:T(8,128)(2,1)S(1)}, bf16[64,256]{1,0:T(8,128)(2,1)S(1)}, u32[]{:S(2)}, u32[]{:S(2)}) collective-permute-start(bf16[64,256]{1,0:T(8,128)(2,1)S(1)} %pad_maximum_fusion.13), channel_id=1, source_target_pairs={{0,16},{8,24},{16,0},{24,8},{32,48},{40,56},{48,32},{56,40},{64,80... | collective-permute-start | bytes 98312 | tf_op jit(solution)/shard_map/ppermute | solution.py:13
  49.7 12.3 %collective-permute-start.10 = (bf16[128,256]{1,0:T(8,128)(2,1)S(1)}, bf16[128,256]{1,0:T(8,128)(2,1)S(1)}, u32[]{:S(2)}, u32[]{:S(2)}) collective-permute-start(bf16[128,256]{1,0:T(8,128)(2,1)S(1)} %pad_maximum_fusion.11), channel_id=1, source_target_pairs={{0,16},{8,24},{16,0},{24,8},{32,48},{40,56},{48,32},{56,40},{64,80... | collective-permute-start | bytes 196616 | tf_op jit(solution)/shard_map/ppermute | solution.py:13
  52.4 14.8 %collective-permute-start.16 = (bf16[128,256]{1,0:T(8,128)(2,1)S(1)}, bf16[128,256]{1,0:T(8,128)(2,1)S(1)}, u32[]{:S(2)}, u32[]{:S(2)}) collective-permute-start(bf16[128,256]{1,0:T(8,128)(2,1)S(1)} %pad_maximum_fusion.12), channel_id=1, source_target_pairs={{0,32},{8,40},{16,48},{24,56},{32,0},{40,8},{48,16},{56,24},{64,96... | collective-permute-start | bytes 196616 | tf_op jit(solution)/shard_map/ppermute | solution.py:13
  59.6 14.4 %collective-permute-start.6 = (bf16[256,256]{1,0:T(8,128)(2,1)S(1)}, bf16[256,256]{1,0:T(8,128)(2,1)S(1)}, u32[]{:S(2)}, u32[]{:S(2)}) collective-permute-start(bf16[256,256]{1,0:T(8,128)(2,1)S(1)} %pad_maximum_fusion.8), channel_id=1, source_target_pairs={{0,16},{8,24},{16,0},{24,8},{32,48},{40,56},{48,32},{56,40},{64,80... | collective-permute-start | bytes 393224 | tf_op jit(solution)/shard_map/ppermute | solution.py:13
  62.0 18.6 %collective-permute-start.11 = (bf16[256,256]{1,0:T(8,128)(2,1)S(1)}, bf16[256,256]{1,0:T(8,128)(2,1)S(1)}, u32[]{:S(2)}, u32[]{:S(2)}) collective-permute-start(bf16[256,256]{1,0:T(8,128)(2,1)S(1)} %pad_maximum_fusion.9), channel_id=1, source_target_pairs={{0,32},{8,40},{16,48},{24,56},{32,0},{40,8},{48,16},{56,24},{64,96... | collective-permute-start | bytes 393224 | tf_op jit(solution)/shard_map/ppermute | solution.py:13
  67.2 16.1 %collective-permute-start.17 = (bf16[256,256]{1,0:T(8,128)(2,1)S(1)}, bf16[256,256]{1,0:T(8,128)(2,1)S(1)}, u32[]{:S(2)}, u32[]{:S(2)}) collective-permute-start(bf16[256,256]{1,0:T(8,128)(2,1)S(1)} %pad_maximum_fusion.10), channel_id=1, source_target_pairs={{0,64},{8,72},{16,80},{24,88},{32,96},{40,104},{48,112},{56,120},{... | collective-permute-start | bytes 393224 | tf_op jit(solution)/shard_map/ppermute | solution.py:13
  71.9 11.4 %copy-start.18 = (bf16[512,256]{1,0:T(8,128)(2,1)S(1)}, bf16[512,256]{1,0:T(8,128)(2,1)}, u32[]{:S(2)}) copy-start(bf16[512,256]{1,0:T(8,128)(2,1)} %get-tuple-element.39) | copy-start | bytes 786436
  71.9 27.7 %collective-permute-start.3 = (bf16[512,256]{1,0:T(8,128)(2,1)S(1)}, bf16[512,256]{1,0:T(8,128)(2,1)S(1)}, u32[]{:S(2)}, u32[]{:S(2)}) collective-permute-start(bf16[512,256]{1,0:T(8,128)(2,1)S(1)} %pad_maximum_fusion.5), channel_id=1, source_target_pairs={{0,16},{8,24},{16,0},{24,8},{32,48},{40,56},{48,32},{56,40},{64,80... | collective-permute-start | bytes 786440 | tf_op jit(solution)/shard_map/ppermute | solution.py:13
  74.0 31.4 %collective-permute-start.7 = (bf16[512,256]{1,0:T(8,128)(2,1)S(1)}, bf16[512,256]{1,0:T(8,128)(2,1)S(1)}, u32[]{:S(2)}, u32[]{:S(2)}) collective-permute-start(bf16[512,256]{1,0:T(8,128)(2,1)S(1)} %pad_maximum_fusion.6), channel_id=1, source_target_pairs={{0,32},{8,40},{16,48},{24,56},{32,0},{40,8},{48,16},{56,24},{64,96... | collective-permute-start | bytes 786440 | tf_op jit(solution)/shard_map/ppermute | solution.py:13
  80.7 27.6 %collective-permute-start.12 = (bf16[512,256]{1,0:T(8,128)(2,1)S(1)}, bf16[512,256]{1,0:T(8,128)(2,1)S(1)}, u32[]{:S(2)}, u32[]{:S(2)}) collective-permute-start(bf16[512,256]{1,0:T(8,128)(2,1)S(1)} %pad_maximum_fusion.7), channel_id=1, source_target_pairs={{0,64},{8,72},{16,80},{24,88},{32,96},{40,104},{48,112},{56,120},{... | collective-permute-start | bytes 786440 | tf_op jit(solution)/shard_map/ppermute | solution.py:13
  84.1 28.9 %collective-permute-start.18 = (bf16[512,256]{1,0:T(8,128)(2,1)S(1)}, bf16[512,256]{1,0:T(8,128)(2,1)S(1)}, u32[]{:S(2)}, u32[]{:S(2)}) collective-permute-start(bf16[512,256]{1,0:T(8,128)(2,1)S(1)} %get-tuple-element.34), channel_id=1, source_target_pairs={{0,128},{8,136},{16,144},{24,152},{32,160},{40,168},{48,176},{56,1... | collective-permute-start | bytes 786440 | tf_op jit(solution)/shard_map/ppermute | solution.py:13
  89.9 27.7 %collective-permute-start.1 = (bf16[1024,256]{1,0:T(8,128)(2,1)S(1)}, bf16[1024,256]{1,0:T(8,128)(2,1)S(1)}, u32[]{:S(2)}, u32[]{:S(2)}) collective-permute-start(bf16[1024,256]{1,0:T(8,128)(2,1)S(1)} %pad_maximum_fusion.2), channel_id=1, source_target_pairs={{0,16},{8,24},{16,0},{24,8},{32,48},{40,56},{48,32},{56,40},{64,80... | collective-permute-start | bytes 1572872 | tf_op jit(solution)/shard_map/ppermute | solution.py:13
  99.7 31.0 %collective-permute-start.4 = (bf16[1024,256]{1,0:T(8,128)(2,1)S(1)}, bf16[1024,256]{1,0:T(8,128)(2,1)S(1)}, u32[]{:S(2)}, u32[]{:S(2)}) collective-permute-start(bf16[1024,256]{1,0:T(8,128)(2,1)S(1)} %pad_maximum_fusion.3), channel_id=1, source_target_pairs={{0,32},{8,40},{16,48},{24,56},{32,0},{40,8},{48,16},{56,24},{64,96... | collective-permute-start | bytes 1572872 | tf_op jit(solution)/shard_map/ppermute | solution.py:13
  106.3 29.2 %collective-permute-start.8 = (bf16[1024,256]{1,0:T(8,128)(2,1)}, bf16[1024,256]{1,0:T(8,128)(2,1)}, u32[]{:S(2)}, u32[]{:S(2)}) collective-permute-start(bf16[1024,256]{1,0:T(8,128)(2,1)} %pad_maximum_fusion.4), channel_id=1, source_target_pairs={{0,64},{8,72},{16,80},{24,88},{32,96},{40,104},{48,112},{56,120},{... | collective-permute-start | bytes 1572872 | tf_op jit(solution)/shard_map/ppermute | solution.py:13
  108.3 12.3 %copy-start.5 = (bf16[2048,256]{1,0:T(8,128)(2,1)}, bf16[2048,256]{1,0:T(8,128)(2,1)S(1)}, u32[]{:S(2)}) copy-start(bf16[2048,256]{1,0:T(8,128)(2,1)S(1)} %constant_dynamic-update-slice_fusion.1) | copy-start | bytes 3145732
  109.2 33.9 %collective-permute-start.13 = (bf16[1024,256]{1,0:T(8,128)(2,1)}, bf16[1024,256]{1,0:T(8,128)(2,1)}, u32[]{:S(2)}, u32[]{:S(2)}) collective-permute-start(bf16[1024,256]{1,0:T(8,128)(2,1)} %get-tuple-element.26), channel_id=1, source_target_pairs={{0,128},{8,136},{16,144},{24,152},{32,160},{40,168},{48,176},{56,1... | collective-permute-start | bytes 1572872 | tf_op jit(solution)/shard_map/ppermute | solution.py:13
  113.8 39.3 %collective-permute-start.19 = (bf16[1024,256]{1,0:T(8,128)(2,1)}, bf16[1024,256]{1,0:T(8,128)(2,1)}, u32[]{:S(2)}, u32[]{:S(2)}) collective-permute-start(bf16[1024,256]{1,0:T(8,128)(2,1)} %get-tuple-element.28), channel_id=1, source_target_pairs={{0,256},{8,264},{16,272},{24,280},{32,288},{40,296},{48,304},{56,3... | collective-permute-start | bytes 1572872 | tf_op jit(solution)/shard_map/ppermute | solution.py:13
  117.7 1.0 copy-start.3
  118.7 2.0 copy-start.1
  118.7 20.5 %copy-start.12 = (f32[512]{0:T(512)}, f32[512]{0:T(512)S(1)}, u32[]{:S(2)}) copy-start(f32[512]{0:T(512)S(1)} %get-tuple-element.63) | copy-start | bytes 6148
  120.7 11.1 %copy-start.9 = (bf16[256,1,128]{2,1,0:T(2,128)(2,1)S(1)}, bf16[256,1,128]{2,1,0:T(2,128)(2,1)}, u32[]{:S(2)}) copy-start(bf16[256,1,128]{2,1,0:T(2,128)(2,1)} %constant_dynamic-slice_fusion.7) | copy-start | bytes 196612
  130.8 1.0 copy-start.2
  132.6 6.6 %copy-start.13 = (f32[512]{0:T(512)}, f32[512]{0:T(512)S(1)}, u32[]{:S(2)}) copy-start(f32[512]{0:T(512)S(1)} %broadcast_in_dim.316) | copy-start | bytes 6148
  133.0 4.5 %copy-start.10 = (bf16[128,1,128]{2,1,0:T(2,128)(2,1)S(1)}, bf16[128,1,128]{2,1,0:T(2,128)(2,1)}, u32[]{:S(2)}) copy-start(bf16[128,1,128]{2,1,0:T(2,128)(2,1)} %constant_dynamic-slice_fusion.5) | copy-start | bytes 98308
  133.8 1.7 copy-start.6
  135.5 3.8 %copy-start.15 = (pred[512]{0:T(512)(128)(4,1)S(1)}, pred[512]{0:T(512)(128)(4,1)}, u32[]{:S(2)}) copy-start(pred[512]{0:T(512)(128)(4,1)} %broadcast_in_dim.314) | copy-start | bytes 1540
  135.5 3.8 %copy-start.16 = (pred[512]{0:T(512)(128)(4,1)S(1)}, pred[512]{0:T(512)(128)(4,1)}, u32[]{:S(2)}) copy-start(pred[512]{0:T(512)(128)(4,1)} %broadcast_in_dim.321) | copy-start | bytes 1540
  136.6 1.0 copy-start.7
  137.9 7.1 %copy-start.11 = (bf16[64,1,128]{2,1,0:T(2,128)(2,1)S(1)}, bf16[64,1,128]{2,1,0:T(2,128)(2,1)}, u32[]{:S(2)}) copy-start(bf16[64,1,128]{2,1,0:T(2,128)(2,1)} %constant_dynamic-slice_fusion.3) | copy-start | bytes 49156
  138.4 9.1 %copy-start.14 = (f32[512]{0:T(512)}, f32[512]{0:T(512)S(1)}, u32[]{:S(2)}) copy-start(f32[512]{0:T(512)S(1)} %broadcast_in_dim.323) | copy-start | bytes 6148
  143.1 10.1 %copy-start.8 = (bf16[2048,256]{1,0:T(8,128)(2,1)S(1)}, bf16[2048,256]{1,0:T(8,128)(2,1)}, u32[]{:S(2)}) copy-start(bf16[2048,256]{1,0:T(8,128)(2,1)} %get-tuple-element.29) | copy-start | bytes 3145732
  150.2 10.3 %copy-start.4 = (bf16[2048,256]{1,0:T(8,128)(2,1)S(1)}, bf16[2048,256]{1,0:T(8,128)(2,1)}, u32[]{:S(2)}) copy-start(bf16[2048,256]{1,0:T(8,128)(2,1)} %copy-done.3) | copy-start | bytes 3145732
Sparse Core Ops, SparseCore 0:
  165.3 91.9 reduce-scatter.1
where the time goes:
time: 266 us; the launch traced here: 264 us
  waiting for transfers between devices  112 us (42%)
  starting transfers between devices  72.1 us (27%)
  local copies, waits for them, and re-layouts  28.4 us (11%)
  between operations  22.2 us (8%)
  matrix products  15.7 us (6%)
  other arithmetic  13.2 us (5%)
    reduce_scatter x1, waiting for transfers between devices, on_device(): lax.psum_scatter(jnp.dot(outputs, w_out, preferred_element_type=jnp.float...  92.2 us
    ppermute x20, starting transfers between devices, partner(): lax.ppermute(x, axis, [(i, i ^ 1 << stride) for i in range(lax.axis_size(...  72.1 us
    ppermute x20, waiting for transfers between devices, partner(): lax.ppermute(x, axis, [(i, i ^ 1 << stride) for i in range(lax.axis_size(...  20.3 us
    unnamed x54, local copies, waits for them, and re-layouts  10.8 us
    broadcast_in_dim x26, local copies, waits for them, and re-layouts, restore(): filled = jnp.where(onehot, expanded, jnp.zeros_like(expanded))  8.08 us
    concatenate x5, local copies, waits for them, and re-layouts, spread(): buffer = jnp.concatenate([buffer, partner_rows], axis=0)  5.93 us
    dot_general x4, matrix products, attend(): jnp.dot(expo.astype(jnp.bfloat16), key_values[:, head_dim:], preferred_el...  5.86 us
  transfers between devices with their start and end apart: 21, of which 4 were waited for; matrix products, arithmetic and copies ran while one was open for 15% of the time, Pallas kernels for 0%

commit v1 on v0

v1 whole, which is shorter than its diff:
```python
import math

import jax
import jax.numpy as jnp
from jax import lax
from jax.experimental import pallas as pl
from jax.experimental.pallas import tpu as pltpu
from jax.sharding import PartitionSpec as P

HD = 128
NB = 5
RING = 8
LINES = 8
HEADS = 8
ROWS = 512
CHUNKS = 4
CH = ROWS // CHUNKS
RES = 16
PICK = [ROWS >> b for b in range(NB)]
Q4, Q3, Q2 = PICK[4], PICK[3], PICK[2]
QTOT = Q4 + Q3 + Q2
COEF = math.log2(math.e) / math.sqrt(HD)
MESH = pl.DeviceIdType.MESH
BF = jnp.bfloat16
F32 = jnp.float32


BASE = {4: 0, 3: Q4, 2: Q4 + Q3, 1: QTOT}


def prefix(j):
    return QTOT if j == 1 else (Q4 + Q3 if j < 4 else Q4)


def xor(a, j):
    out = 0
    for bit in range(3):
        low = lax.rem(lax.div(a, 1 << bit), 2)
        out = out + ((1 - low) if (j >> bit) & 1 else low) * (1 << bit)
    return out


def home(i):
    g, k = i // 32, i % 32
    res = (g % 2) * 8 + (g // 2 % 2) * 4 + (g // 4 % 2) * 2 + g // 8
    return k * RES + res


def mat(a, b):
    return jnp.dot(a, b, preferred_element_type=F32)


def attend(q, k, v):
    s = lax.dot_general(q, k, (((1,), (1,)), ((), ())), preferred_element_type=F32)
    m = jnp.max(s, axis=1, keepdims=True)
    p = jnp.exp2((s - m) * COEF)
    l = jnp.sum(p, axis=1, keepdims=True)
    return m, l, mat(p.astype(BF), v)


def join(parts):
    top = parts[0][0]
    for m, _, _ in parts[1:]:
        top = jnp.maximum(top, m)
    den, num = 0.0, 0.0
    for m, l, a in parts:
        w = jnp.exp2((m - top) * COEF)
        den = den + w * l
        num = num + w * a
    return top, den, num


def three(x):
    hi = x.astype(BF).astype(F32)
    mid = (x - hi).astype(BF).astype(F32)
    return hi, mid, x - hi - mid


def pack(m, l):
    lane = lax.broadcasted_iota(jnp.int32, (m.shape[0], HD), 1)
    out = jnp.zeros((m.shape[0], HD), F32)
    for i, part in enumerate(three(m) + three(l)):
        out = jnp.where(lane == i, part, out)
    return out.astype(BF)


def unpack(block):
    a = block[:, :HD].astype(F32)
    t = block[:, HD:].astype(F32)
    m = t[:, 0:1] + (t[:, 1:2] + t[:, 2:3])
    l = t[:, 3:4] + (t[:, 4:5] + t[:, 5:6])
    return m, l, a


def kernel(
    off_ref, tok_ref, wqkv_ref, wout_ref, out_ref,
    own, r1, l1, r2, l2, r3, l3, far,
    sel, kb0, kb1, kb2, kb3, kb4, qb, qs, rq, ps, ro, att, ag, wf, acc0, st0,
    ysend, yrecv, qsend, qrecv, psend, precv, wsend, wrecv, asend, arecv,
):
    s_idx = lax.axis_index("seq")
    h = lax.axis_index("head")
    z, y = lax.div(s_idx, RING), lax.rem(s_idx, RING)
    x, core = lax.div(h, 2), lax.rem(h, 2)

    def at_y(d):
        return z * RING + lax.rem(y + RING + d, RING)

    def at_z(j):
        return xor(z, j) * RING + y

    barrier = pltpu.get_barrier_semaphore()
    peers = [(at_y(-1), h), (at_y(1), h)]
    peers += [(at_z(j), h) for j in range(1, LINES)]
    peers += [(s_idx, xor(h, j)) for j in range(1, HEADS)]
    for peer in peers:
        pl.semaphore_signal(barrier, inc=1, device_id=peer, device_id_type=MESH)

    def remote(src, dst, send, recv, peer):
        return pltpu.make_async_remote_copy(
            src_ref=src, dst_ref=dst, send_sem=send, recv_sem=recv,
            device_id=peer, device_id_type=MESH,
        )

    starts = []
    for b in range(1, NB):
        o = off_ref[b, h]
        rev = 0
        for bit in range(b):
            rev = rev * 2 + lax.rem(lax.div(o, 1 << bit), 2)
        starts.append(rev * PICK[b])

    rowi = lax.broadcasted_iota(jnp.int32, (ROWS, ROWS), 0)
    coli = lax.broadcasted_iota(jnp.int32, (ROWS, ROWS), 1)
    perm = jnp.where(home(rowi) == coli, 1.0, 0.0).astype(BF)
    for b in range(NB - 1, 0, -1):
        n = PICK[b]
        hit = rowi[:n] + starts[b - 1] == coli[:n]
        sel[BASE[b] : BASE[b] + n] = jnp.where(hit, 1.0, 0.0).astype(BF)

    kv = mat(tok_ref[...], wqkv_ref[:, HD:]).astype(BF)
    own[...] = mat(perm, kv).astype(BF)
    pl.semaphore_wait(barrier, len(peers))

    flows = [
        ([own, r1, r2, r3], [r1, r2, r3, far], (at_y(-1), h)),
        ([own, l1, l2, l3], [l1, l2, l3, far], (at_y(1), h)),
    ]

    def ring(d, hop, c):
        src, dst, peer = flows[d]
        rows = pl.ds(c * CH, CH)
        return remote(
            src[hop].at[rows], dst[hop].at[rows], ysend.at[d, hop, c], yrecv.at[d, hop, c], peer
        )

    def last(d):
        return range(CHUNKS // 2) if d == 0 else range(CHUNKS // 2, CHUNKS)

    sends = []
    for c in range(CHUNKS):
        for d in range(2):
            copy = ring(d, 0, c)
            copy.start()
            sends.append(copy)

    wcopies = []
    for dx in range(1, 4):
        copy = remote(
            wout_ref, wf.at[h], wsend.at[dx], wrecv.at[dx],
            (s_idx, lax.rem(x + dx, 4) * 2 + core),
        )
        copy.start()
        wcopies.append(copy)
    sibling = (s_idx, x * 2 + 1 - core)
    pair = remote(wout_ref, wf.at[h], wsend.at[0], wrecv.at[0], sibling)
    pair.start()

    q = mat(tok_ref[...], wqkv_ref[:, :HD]).astype(BF)
    qb[...] = mat(perm, q).astype(BF)
    qs[...] = mat(sel[...], qb[...]).astype(BF)
    qcopies = []
    for j in range(1, LINES):
        n = prefix(j)
        copy = remote(
            qs.at[pl.ds(0, n)], rq.at[j, pl.ds(0, n)], qsend.at[j], qrecv.at[j], (at_z(j), h)
        )
        copy.start()
        qcopies.append(copy)
    wf[h] = wout_ref[...]

    def take(ref, slot, place):
        kb0[place] = ref[...]
        taken = mat(sel[...], ref[...]).astype(BF)
        for b, buf in ((1, kb1), (2, kb2), (3, kb3), (4, kb4)):
            n = PICK[b]
            buf[slot * n : (slot + 1) * n] = taken[BASE[b] : BASE[b] + n]

    take(own, 0, y)

    def arrive(hop):
        for c in range(CHUNKS):
            for d in range(2):
                ring(d, hop, c).wait_recv()
                if hop < 2 or c in last(d):
                    copy = ring(d, hop + 1, c)
                    copy.start()
                    sends.append(copy)

    arrive(0)
    take(r1, 1, lax.rem(y + 1, RING))
    take(l1, 2, lax.rem(y + 7, RING))
    arrive(1)
    take(r2, 3, lax.rem(y + 2, RING))
    take(l2, 4, lax.rem(y + 6, RING))

    relays = []
    for dx in range(1, 4):
        wcopies[dx - 1].wait_recv()
        slot = lax.rem(x + 4 - dx, 4) * 2 + core
        copy = remote(wf.at[slot], wf.at[slot], wsend.at[3 + dx], wrecv.at[3 + dx], sibling)
        copy.start()
        relays.append(copy)

    for copy in qcopies:
        copy.wait_recv()
    q1 = qs[QTOT : QTOT + PICK[1]]
    q2 = jnp.concatenate([qs[Q4 + Q3 : QTOT]] + [rq[1, Q4 + Q3 : QTOT]], axis=0)
    q3 = jnp.concatenate([qs[Q4 : Q4 + Q3]] + [rq[j, Q4 : Q4 + Q3] for j in range(1, 4)], axis=0)
    q4 = jnp.concatenate([qs[0:Q4]] + [rq[j, 0:Q4] for j in range(1, LINES)], axis=0)
    small = [(q1, kb1, PICK[1]), (q2, kb2, Q2), (q3, kb3, Q3), (q4, kb4, Q4)]

    arrive(2)
    take(r3, 5, lax.rem(y + 3, RING))
    take(l3, 6, lax.rem(y + 5, RING))
    first = [attend(qq, kb[0 : 7 * n, :HD], kb[0 : 7 * n, HD:]) for qq, kb, n in small]

    for d in range(2):
        for c in last(d):
            ring(d, 3, c).wait_recv()
    take(far, 7, lax.rem(y + 4, RING))
    full = [None] * 4
    for i in (3, 2, 1, 0):
        qq, kb, n = small[i]
        full[i] = join([first[i], attend(qq, kb[7 * n : 8 * n, :HD], kb[7 * n : 8 * n, HD:])])
        if i == 0:
            break
        m, l, a = full[i]
        base = {3: 0, 2: Q4, 1: Q4 + Q3}[i]
        msg = jnp.concatenate([a.astype(BF), pack(m, l)], axis=1)
        for j in range(1, 2 ** i):
            ps[j, base : base + n] = msg[j * n : (j + 1) * n]
        for j in {3: range(4, 8), 2: range(2, 4), 1: range(1, 2)}[i]:
            k = prefix(j)
            copy = remote(
                ps.at[j, pl.ds(0, k)], ro.at[j, pl.ds(0, k)], psend.at[j], precv.at[j], (at_z(j), h)
            )
            copy.start()
            qcopies.append(copy)

    half = lax.div(y, 4) * 4

    def tile(t, carry):
        rows = pl.ds(t * 256, 256)
        keys = kb0[pl.ds(half, 4)].reshape(4 * ROWS, 2 * HD)
        m, l, a = attend(qb[rows, :], keys[:, :HD], keys[:, HD:])
        acc0[rows, :] = a
        st0[0, rows, :] = jnp.broadcast_to(m, (256, HD))
        st0[1, rows, :] = jnp.broadcast_to(l, (256, HD))
        return carry

    lax.fori_loop(0, 2, tile, 0)

    for copy in qcopies[LINES - 1 :]:
        copy.wait_recv()
    own_part = [full[0]]
    for i, base in ((1, Q4 + Q3), (2, Q4), (3, 0)):
        n = PICK[i + 1]
        mine = tuple(v[0:n] for v in full[i])
        own_part.append(join([mine] + [unpack(ro[j, base : base + n]) for j in range(1, 2 ** i)]))

    m0, l0, a0 = st0[0], st0[1], acc0[...]
    rows = lax.broadcasted_iota(jnp.int32, (ROWS, HD), 0)
    spread = []
    top = m0
    for b in range(1, NB):
        m, l, a = own_part[b - 1]
        n = PICK[b]
        chosen = (rows >= starts[b - 1]) & (rows < starts[b - 1] + n)
        m = jnp.broadcast_to(m, (n, HD))
        l = jnp.broadcast_to(l, (n, HD))
        m, l, a = (jnp.concatenate([v] * (2 ** b), axis=0) for v in (m, l, a))
        m = jnp.where(chosen, m, m0)
        top = jnp.maximum(top, m)
        spread.append((chosen, m, l, a))
    w = jnp.exp2((m0 - top) * COEF)
    den, num = w * l0, w * a0
    for chosen, m, l, a in spread:
        w = jnp.where(chosen, jnp.exp2((m - top) * COEF), 0.0)
        den = den + w * l
        num = num + w * a
    attended = (num / den).astype(BF)
    back = jnp.where(home(coli) == rowi, 1.0, 0.0).astype(BF)
    att[...] = mat(back, attended).astype(BF)

    piece = ROWS // HEADS
    acopies = []
    for j in range(1, HEADS):
        to = xor(h, j)
        copy = remote(
            att.at[pl.ds(pl.multiple_of(to * piece, piece), piece)], ag.at[h],
            asend.at[j], arecv.at[j], (s_idx, to),
        )
        copy.start()
        acopies.append(copy)
    ag[h] = att[pl.ds(pl.multiple_of(h * piece, piece), piece), :]
    pair.wait_recv()
    for copy in relays:
        copy.wait_recv()
    for copy in acopies:
        copy.wait_recv()
    lhs = jnp.concatenate([ag[i] for i in range(HEADS)], axis=1)
    out_ref[...] = mat(lhs, wf[...].reshape(HEADS * HD, HEADS * HD)).astype(BF)
    for copy in sends + wcopies + [pair] + relays + qcopies + acopies:
        copy.wait_send()


def on_device(tokens, w_qkv, w_out, offsets):
    vmem = pl.BlockSpec(memory_space=pltpu.VMEM)
    dma = pltpu.SemaphoreType.DMA
    block = pltpu.VMEM((ROWS, 2 * HD), BF)
    return pl.pallas_call(
        kernel,
        out_shape=jax.ShapeDtypeStruct((ROWS // HEADS, HEADS * HD), BF),
        in_specs=[pl.BlockSpec(memory_space=pltpu.SMEM), vmem, vmem, vmem],
        out_specs=vmem,
        scratch_shapes=[block] * 8
        + [pltpu.VMEM((QTOT + PICK[1], ROWS), BF), pltpu.VMEM((RING, ROWS, 2 * HD), BF)]
        + [pltpu.VMEM((RING * PICK[b], 2 * HD), BF) for b in range(1, NB)]
        + [
            pltpu.VMEM((ROWS, HD), BF),
            pltpu.VMEM((QTOT + PICK[1], HD), BF),
            pltpu.VMEM((LINES, QTOT, HD), BF),
            pltpu.VMEM((LINES, QTOT, 2 * HD), BF),
            pltpu.VMEM((LINES, QTOT, 2 * HD), BF),
            pltpu.VMEM((ROWS, HD), BF),
            pltpu.VMEM((HEADS, ROWS // HEADS, HD), BF),
            pltpu.VMEM((HEADS, HD, HEADS * HD), BF),
            pltpu.VMEM((ROWS, HD), F32),
            pltpu.VMEM((2, ROWS, HD), F32),
        ]
        + [dma((2, 4, CHUNKS))] * 2
        + [dma((LINES,))] * 4
        + [dma((7,))] * 2
        + [dma((HEADS,))] * 2,
        compiler_params=pltpu.CompilerParams(
            collective_id=0, has_side_effects=True, vmem_limit_bytes=50 * 1024 * 1024
        ),
    )(offsets, tokens, w_qkv, w_out)


def solution(mesh):
    in_specs = (P("seq", None), P(None, "head"), P("head", None), P())
    out_specs = P(("seq", "head"), None)
    return jax.shard_map(
        on_device, mesh=mesh, in_specs=in_specs, out_specs=out_specs, check_vma=False
    )
```

time: 266 us -> 57 us (0.21)
  waiting for transfers between devices: 112 us -> 0 us
  starting transfers between devices: 72.1 us -> 0 us
  Pallas kernels: 0 us -> 52.1 us
  local copies, waits for them, and re-layouts: 28.4 us -> 4.65 us
  between operations: 22.2 us -> 0.01 us
  matrix products: 15.7 us -> 0 us
  other arithmetic: 13.2 us -> 0 us
    reduce_scatter x1 -> x0, waiting for transfers between devices: 92.2 us -> none  [on_device(): lax.psum_scatter(jnp.dot(outputs, w_out, preferred_element_type=jnp.float...]
    ppermute x20 -> x0, starting transfers between devices: 72.1 us -> none  [partner(): lax.ppermute(x, axis, [(i, i ^ 1 << stride) for i in range(lax.axis_size(...]
    pallas_call x0 -> x1, Pallas kernels: none -> 52.1 us  [on_device(): pl.pallas_call(kernel, out_shape=jax.ShapeDtypeStruct((ROWS // HEADS, HEA...]
    ppermute x20 -> x0, waiting for transfers between devices: 20.3 us -> none  [partner(): lax.ppermute(x, axis, [(i, i ^ 1 << stride) for i in range(lax.axis_size(...]
    dot_general x11 -> x0, matrix products: 15.7 us -> none  [the longest x4 5.86 us: attend(): jnp.dot(expo.astype(jnp.bfloat16), key_values[:, head_dim:], preferred_el...]
    broadcast_in_dim x26 -> x0, local copies, waits for them, and re-layouts: 8.08 us -> none  [restore(): filled = jnp.where(onehot, expanded, jnp.zeros_like(expanded))]
    unnamed x54 -> x9, local copies, waits for them, and re-layouts: 10.8 us -> 4.65 us
    concatenate x5 -> x0, local copies, waits for them, and re-layouts: 5.93 us -> none  [spread(): buffer = jnp.concatenate([buffer, partner_rows], axis=0)]
  transfers between devices with their start and end apart: 21 -> 0, of which waited for: 4 -> 0; matrix products, arithmetic and copies ran while one was open for 15% -> 0% of each run, Pallas kernels for 0% -> 0%
where the time goes in v1:
time: 57 us; the launch traced here: 56.7 us
  Pallas kernels  52.1 us (91%)
  local copies, waits for them, and re-layouts  4.65 us (8%)
    pallas_call x1, Pallas kernels, on_device(): pl.pallas_call(kernel, out_shape=jax.ShapeDtypeStruct((ROWS // HEADS, HEA...  52.1 us
    unnamed x9, local copies, waits for them, and re-layouts  4.65 us

profile of v1, /device:TPU:1, one launch (start us, length us, event | category | flops | bytes accessed | tf_op | source)
XLA Modules:
  0.0 56.7 jit_solution(13931241361173018984)
XLA Ops:
  0.0 0.0 copy-start
  0.0 1.2 %copy-done = bf16[512,1024]{1,0:T(8,128)(2,1)S(1)} copy-done((bf16[512,1024]{1,0:T(8,128)(2,1)S(1)}, bf16[512,1024]{1,0:T(8,128)(2,1)}, u32[]{:S(2)}) %copy-start) | copy-done | bytes 1048600
  1.2 0.0 copy-start.1
  1.2 1.1 %copy-done.1 = bf16[1024,384]{1,0:T(8,128)(2,1)S(1)} copy-done((bf16[1024,384]{1,0:T(8,128)(2,1)S(1)}, bf16[1024,384]{1,0:T(8,128)(2,1)}, u32[]{:S(2)}) %copy-start.1) | copy-done | bytes 786456
  2.4 0.0 copy-start.2
  2.4 0.9 %copy-done.2 = bf16[128,1024]{1,0:T(8,128)(2,1)S(1)} copy-done((bf16[128,1024]{1,0:T(8,128)(2,1)S(1)}, bf16[128,1024]{1,0:T(8,128)(2,1)}, u32[]{:S(2)}) %copy-start.2) | copy-done | bytes 262168
  3.3 0.0 copy-start.3
  3.3 0.7 %copy-done.3 = s32[5,8]{1,0:T(8,128)S(1)} copy-done((s32[5,8]{1,0:T(8,128)S(1)}, s32[5,8]{1,0:T(8,128)}, u32[]{:S(2)}) %copy-start.3) | copy-done | bytes 184
  4.0 52.1 %shard_map.46 = bf16[64,1024]{1,0:T(8,128)(2,1)S(1)} custom-call(s32[5,8]{1,0:T(8,128)S(1)} %copy-done.3, bf16[512,1024]{1,0:T(8,128)(2,1)S(1)} %copy-done, bf16[1024,384]{1,0:T(8,128)(2,1)S(1)} %copy-done.1, bf16[128,1024]{1,0:T(8,128)(2,1)S(1)} %copy-done.2), custom_call_target="tpu_custom_call" | custom-call | tf_op jit(solution)/shard_map/pallas_call | solution.py:332
  56.1 0.7 %copy.6 = bf16[64,1024]{1,0:T(8,128)(2,1)} copy(bf16[64,1024]{1,0:T(8,128)(2,1)S(1)} %shard_map.46) | data formatting | bytes 262144
Async XLA Ops:
  0.0 1.2 %copy-start = (bf16[512,1024]{1,0:T(8,128)(2,1)S(1)}, bf16[512,1024]{1,0:T(8,128)(2,1)}, u32[]{:S(2)}) copy-start(bf16[512,1024]{1,0:T(8,128)(2,1)} %tok_ref.1) | copy-start | bytes 3145732
  1.2 1.1 %copy-start.1 = (bf16[1024,384]{1,0:T(8,128)(2,1)S(1)}, bf16[1024,384]{1,0:T(8,128)(2,1)}, u32[]{:S(2)}) copy-start(bf16[1024,384]{1,0:T(8,128)(2,1)} %wqkv_ref.1) | copy-start | bytes 2359300
  2.4 0.9 %copy-start.2 = (bf16[128,1024]{1,0:T(8,128)(2,1)S(1)}, bf16[128,1024]{1,0:T(8,128)(2,1)}, u32[]{:S(2)}) copy-start(bf16[128,1024]{1,0:T(8,128)(2,1)} %wout_ref.1) | copy-start | bytes 786436
  3.3 0.7 %copy-start.3 = (s32[5,8]{1,0:T(8,128)S(1)}, s32[5,8]{1,0:T(8,128)}, u32[]{:S(2)}) copy-start(s32[5,8]{1,0:T(8,128)} %off_ref.1) | copy-start | bytes 484

commit v2 on v1

v2 whole, which is shorter than its diff:
```python
import math

import jax
import jax.numpy as jnp
from jax import lax
from jax.experimental import pallas as pl
from jax.experimental.pallas import tpu as pltpu
from jax.sharding import PartitionSpec as P

HD = 128
NB = 5
RING = 8
LINES = 8
HEADS = 8
ROWS = 512
RES = 16
BLK = 128
NBLK = ROWS // BLK
HALF = ROWS // 2
CHUNKS = NBLK
CH = HALF // CHUNKS
PICK = [ROWS >> b for b in range(NB)]
PER = [BLK >> b for b in range(NB)]
Q4, Q3, Q2, Q1 = PICK[4], PICK[3], PICK[2], PICK[1]
QTOT = Q4 + Q3 + Q2
BASE = {4: 0, 3: Q4, 2: Q4 + Q3, 1: QTOT}
COEF = math.log2(math.e) / math.sqrt(HD)
MESH = pl.DeviceIdType.MESH
BF = jnp.bfloat16
F32 = jnp.float32
I32 = jnp.int32


def prefix(j):
    return QTOT if j == 1 else (Q4 + Q3 if j < 4 else Q4)


def xor(a, j):
    out = 0
    for bit in range(3):
        low = lax.rem(lax.div(a, 1 << bit), 2)
        out = out + ((1 - low) if (j >> bit) & 1 else low) * (1 << bit)
    return out


def iota(shape, dim):
    return lax.broadcasted_iota(I32, shape, dim)


def home(i):
    g, k = i >> 3, i & 7
    res = ((g & 1) << 3) | ((g & 2) << 1) | ((g & 4) >> 1) | (g >> 3)
    return k * RES + res


def onehot(a, b):
    return jnp.where(a == b, 1.0, 0.0).astype(BF)


def mat(a, b):
    return jnp.dot(a, b, preferred_element_type=F32)


def attend(q, kv):
    s = lax.dot_general(q, kv[:, :HD], (((1,), (1,)), ((), ())), preferred_element_type=F32)
    m = jnp.max(s, axis=1, keepdims=True)
    p = jnp.exp2((s - m) * COEF)
    l = jnp.sum(p, axis=1, keepdims=True)
    return m, l, mat(p.astype(BF), kv[:, HD:])


def join(parts):
    top = parts[0][0]
    for m, _, _ in parts[1:]:
        top = jnp.maximum(top, m)
    den, num = 0.0, 0.0
    for m, l, a in parts:
        w = jnp.exp2((m - top) * COEF)
        den = den + w * l
        num = num + w * a
    return top, den, num


def three(x):
    hi = x.astype(BF).astype(F32)
    mid = (x - hi).astype(BF).astype(F32)
    return hi, mid, x - hi - mid


def pack(m, l):
    lane = iota((m.shape[0], HD), 1)
    out = jnp.zeros((m.shape[0], HD), F32)
    for i, part in enumerate(three(m) + three(l)):
        out = jnp.where(lane == i, part, out)
    return out.astype(BF)


def unpack(block):
    a = block[:, :HD].astype(F32)
    t = block[:, HD:].astype(F32)
    m = t[:, 0:1] + (t[:, 1:2] + t[:, 2:3])
    l = t[:, 3:4] + (t[:, 4:5] + t[:, 5:6])
    return m, l, a


def kernel(
    off_hbm, tok_hbm, wqkv_hbm, wout_hbm, out_ref,
    off, tok, wkv, wq, wout, rings, selq, sela, selb, kb0, kb1, kb2, kb3, kb4, qb, qs, rq, ps, ro,
    att, ag, wf, acc0, st0, res1, res2, res3, res4,
    insem, ysend, yrecv, qsend, qrecv, psend, precv, wsend, wrecv, asend, arecv,
):
    s_idx = lax.axis_index("seq")
    h = lax.axis_index("head")
    z, y = lax.div(s_idx, RING), lax.rem(s_idx, RING)
    x, core = lax.div(h, 2), lax.rem(h, 2)

    loads = [
        (off_hbm, off),
        (wqkv_hbm.at[:, pl.ds(HD, 2 * HD)], wkv),
        *((tok_hbm.at[pl.ds(c * BLK, BLK)], tok.at[pl.ds(c * BLK, BLK)]) for c in range(NBLK)),
        (wqkv_hbm.at[:, pl.ds(0, HD)], wq),
        (wout_hbm, wout),
    ]
    loads = [pltpu.make_async_copy(a, b, insem.at[i]) for i, (a, b) in enumerate(loads)]
    for copy in loads:
        copy.start()

    def at_y(d):
        return z * RING + lax.rem(y + RING + d, RING)

    barrier = pltpu.get_barrier_semaphore()
    peers = [(at_y(-1), h), (at_y(1), h)]
    peers += [(xor(z, j) * RING + y, h) for j in range(1, LINES)]
    peers += [(s_idx, xor(h, j)) for j in range(1, HEADS)]
    for peer in peers:
        pl.semaphore_signal(barrier, inc=1, device_id=peer, device_id_type=MESH)

    def remote(src, dst, send, recv, peer):
        return pltpu.make_async_remote_copy(
            src_ref=src, dst_ref=dst, send_sem=send, recv_sem=recv,
            device_id=peer, device_id_type=MESH,
        )

    loads[0].wait()
    offs = [off[b, h] for b in range(NB)]
    revs = [0]
    for b in range(1, NB):
        rev = 0
        for bit in range(b):
            rev = rev * 2 + lax.rem(lax.div(offs[b], 1 << bit), 2)
        revs.append(rev)
    wanted = []
    for rho in range(RES):
        hit = (offs[4] == rho) | (offs[3] == rho % 8) | (offs[2] == rho % 4)
        wanted.append(jnp.where(hit, 1, 0))
    total = sum(wanted)
    ranks, before = [], 0
    for rho in range(RES):
        ranks.append(before * wanted[rho] + (total + rho - before) * (1 - wanted[rho]))
        before = before + wanted[rho]

    lane = iota((1, BLK), 1)
    rank = jnp.zeros((1, BLK), I32)
    for rho in range(RES):
        rank = jnp.where((lane & 15) == rho, ranks[rho], rank)
    travel = onehot(iota((BLK, 1), 0), rank * 8 + (lane >> 4))
    place = iota((1, ROWS), 1)
    group = ((place >> 3) & 7) + ((place >> 8) << 3)
    label = jnp.zeros((1, ROWS), I32)
    for rho in range(RES):
        label = jnp.where(group == ranks[rho], rho, label)
    label = label * 32 + ((place >> 6) & 3) * 8 + (place & 7)
    for b in range(NB - 1, 0, -1):
        n = PICK[b]
        row = iota((n, 1), 0)
        key = (offs[b] + (row >> 5) * (1 << b)) * 32 + (row & 31)
        if b > 1:
            sela[BASE[b] : BASE[b] + n] = onehot(key, label[:, :HALF])
        else:
            selb[...] = onehot(key, label)
    static = onehot(home(iota((BLK, 1), 0)), iota((1, BLK), 1))
    back = onehot(iota((BLK, 1), 0), home(iota((1, BLK), 1)))

    own, sides, far = 0, [[1, 3, 5], [2, 4, 6]], 7
    flow_peer = [(at_y(-1), h), (at_y(1), h)]

    def ring(ph, d, hop, c):
        slots = [own] + sides[d] + [far]
        rows = pl.ds(c * CH, CH)
        return remote(
            rings.at[ph, slots[hop], rows], rings.at[ph, slots[hop + 1], rows],
            ysend.at[ph, d, hop, c], yrecv.at[ph, d, hop, c], flow_peer[d],
        )

    def last(d):
        return range(CHUNKS // 2) if d == 0 else range(CHUNKS // 2, CHUNKS)

    sends = []

    def send(ph, hop, c):
        for d in range(2):
            if hop < 3 or c in last(d):
                copy = ring(ph, d, hop, c)
                copy.start()
                sends.append(copy)

    def arrive(ph, hop):
        for c in range(CHUNKS):
            for d in range(2):
                if hop < 3 or c in last(d):
                    ring(ph, d, hop, c).wait_recv()
                    if hop < 2 or (hop == 2 and c in last(d)):
                        copy = ring(ph, d, hop + 1, c)
                        copy.start()
                        sends.append(copy)

    loads[1].wait()
    for c in range(NBLK):
        loads[2 + c].wait()
        kv = mat(tok[c * BLK : (c + 1) * BLK], wkv[...]).astype(BF)
        kv = mat(travel, kv).astype(BF)
        rings[0, own, c * CH : (c + 1) * CH] = kv[:CH]
        rings[1, own, c * CH : (c + 1) * CH] = kv[CH:]
        if c == 0:
            pl.semaphore_wait(barrier, len(peers))
        send(0, 0, c)

    loads[6].wait()
    for c in range(NBLK):
        rows = slice(c * BLK, (c + 1) * BLK)
        qb[rows] = mat(static, mat(tok[rows], wq[...]).astype(BF)).astype(BF)
    for b in range(NB - 1, 0, -1):
        n, per = PICK[b], PER[b]
        row = iota((n, 1), 0)
        shift = per.bit_length() - 1
        key = (row >> shift) * BLK + revs[b] * per + (row & (per - 1))
        selq[BASE[b] : BASE[b] + n] = onehot(key, place)
    qs[...] = mat(selq[...], qb[...]).astype(BF)
    qcopies = []
    for j in range(1, LINES):
        n = prefix(j)
        copy = remote(
            qs.at[pl.ds(0, n)], rq.at[j, pl.ds(0, n)], qsend.at[j], qrecv.at[j],
            (xor(z, j) * RING + y, h),
        )
        copy.start()
        qcopies.append(copy)

    loads[7].wait()
    wcopies = []
    for dx in range(1, 4):
        copy = remote(
            wout, wf.at[h], wsend.at[dx], wrecv.at[dx], (s_idx, lax.rem(x + dx, 4) * 2 + core)
        )
        copy.start()
        wcopies.append(copy)
    sibling = (s_idx, x * 2 + 1 - core)
    pair = remote(wout, wf.at[h], wsend.at[0], wrecv.at[0], sibling)
    pair.start()
    wf[h] = wout[...]

    signed = [0, 1, -1, 2, -2, 3, -3, 4]

    def take_a(slot):
        block = rings[0, slot]
        kb0[lax.rem(y + RING + signed[slot], RING), 0:HALF] = block
        taken = mat(sela[...], block).astype(BF)
        for b, buf in ((2, kb2), (3, kb3), (4, kb4)):
            n = PICK[b]
            buf[slot * n : (slot + 1) * n] = taken[BASE[b] : BASE[b] + n]

    def take_b(slot):
        block = rings[1, slot]
        kb0[lax.rem(y + RING + signed[slot], RING), HALF:ROWS] = block
        both = mat(selb[:, :HALF], rings[0, slot]) + mat(selb[:, HALF:], block)
        kb1[slot * Q1 : (slot + 1) * Q1] = both.astype(BF)

    take_a(0)
    arrive(0, 0)
    take_a(1)
    take_a(2)
    arrive(0, 1)
    take_a(3)
    take_a(4)
    arrive(0, 2)
    for c in range(CHUNKS):
        send(1, 0, c)
    take_a(5)
    take_a(6)
    for copy in qcopies:
        copy.wait_recv()
    q1 = qs[QTOT : QTOT + Q1]
    q2 = jnp.concatenate([qs[Q4 + Q3 : QTOT], rq[1, Q4 + Q3 : QTOT]], axis=0)
    q3 = jnp.concatenate([qs[Q4 : Q4 + Q3]] + [rq[j, Q4 : Q4 + Q3] for j in range(1, 4)], axis=0)
    q4 = jnp.concatenate([qs[0:Q4]] + [rq[j, 0:Q4] for j in range(1, LINES)], axis=0)
    arrive(0, 3)
    take_a(far)

    mine = {}
    for b, qq, kb in ((4, q4, kb4), (3, q3, kb3), (2, q2, kb2)):
        m, l, a = attend(qq, kb[...])
        n, base, lines = PICK[b], BASE[b], 1 << (b - 1)
        mine[b] = (m[:n], l[:n], a[:n])
        msg = jnp.concatenate([a.astype(BF), pack(m, l)], axis=1)
        for j in range(1, lines):
            ps[j, base : base + n] = msg[j * n : (j + 1) * n]
        for j in range(lines // 2, lines):
            k = prefix(j)
            copy = remote(
                ps.at[j, pl.ds(0, k)], ro.at[j, pl.ds(0, k)], psend.at[j], precv.at[j],
                (xor(z, j) * RING + y, h),
            )
            copy.start()
            qcopies.append(copy)

    def keep(res, part):
        m, l, a = part
        res[0] = a
        res[1] = jnp.broadcast_to(m, a.shape)
        res[2] = jnp.broadcast_to(l, a.shape)

    take_b(0)
    arrive(1, 0)
    take_b(1)
    take_b(2)
    relays = []
    for dx in range(1, 4):
        wcopies[dx - 1].wait_recv()
        slot = lax.rem(x + 4 - dx, 4) * 2 + core
        copy = remote(wf.at[slot], wf.at[slot], wsend.at[3 + dx], wrecv.at[3 + dx], sibling)
        copy.start()
        relays.append(copy)
    arrive(1, 1)
    take_b(3)
    take_b(4)

    half = lax.div(y, 4) * 4
    upper = lax.div(lax.rem(y, 4), 2)

    def tile(t, carry):
        rows = pl.ds(pl.multiple_of(t * 256, 256), 256)
        keys = kb0[pl.ds(half + upper, 3)].reshape(3 * ROWS, 2 * HD)
        m, l, a = attend(qb[rows, :], keys)
        acc0[rows, :] = a
        st0[0, rows, :] = jnp.broadcast_to(m, (256, HD))
        st0[1, rows, :] = jnp.broadcast_to(l, (256, HD))
        return carry

    def tile2(t, carry):
        rows = pl.ds(pl.multiple_of(t * 256, 256), 256)
        part = attend(qb[rows, :], kb0[half + 3 - 3 * upper])
        m, l, a = join([(st0[0, rows, :], st0[1, rows, :], acc0[rows, :]), part])
        acc0[rows, :] = a
        st0[0, rows, :] = m
        st0[1, rows, :] = l
        return carry

    lax.fori_loop(0, 2, tile, 0)
    first = attend(q1, kb1[0 : 5 * Q1])
    arrive(1, 2)
    take_b(5)
    take_b(6)
    lax.fori_loop(0, 2, tile2, 0)
    second = attend(q1, kb1[5 * Q1 : 7 * Q1])
    for copy in qcopies[LINES - 1 :]:
        copy.wait_recv()
    for b, res in ((2, res2), (3, res3), (4, res4)):
        n, base = PICK[b], BASE[b]
        parts = [unpack(ro[j, base : base + n]) for j in range(1, 1 << (b - 1))]
        keep(res, join([mine[b]] + parts))
    arrive(1, 3)
    take_b(far)
    keep(res1, join([first, second, attend(q1, kb1[7 * Q1 : 8 * Q1])]))

    piece = ROWS // HEADS

    def hand(c, i):
        to = c * 2 + i
        rows = pl.ds(pl.multiple_of(to * piece, piece), piece)
        return remote(att.at[rows], ag.at[h], asend.at[to], arecv.at[h], (s_idx, to))

    def merge(step, carry):
        t = NBLK - 1 - step
        c = lax.rem(x + t + lax.div(t, 2) * (5 - 2 * t), 4)
        rows = pl.ds(pl.multiple_of(c * BLK, BLK), BLK)
        m0, l0, a0 = st0[0, rows, :], st0[1, rows, :], acc0[rows, :]
        place_of = iota((BLK, HD), 0)
        spread = []
        top = m0
        for b, res in ((1, res1), (2, res2), (3, res3), (4, res4)):
            per = PER[b]
            part = pl.ds(pl.multiple_of(c * per, per), per)
            a, m, l = (jnp.concatenate([res[i, part, :]] * (1 << b), axis=0) for i in range(3))
            chosen = (place_of >> (per.bit_length() - 1)) == revs[b]
            m = jnp.where(chosen, m, m0)
            top = jnp.maximum(top, m)
            spread.append((chosen, m, l, a))
        w = jnp.exp2((m0 - top) * COEF)
        den, num = w * l0, w * a0
        for chosen, m, l, a in spread:
            w = jnp.where(chosen, jnp.exp2((m - top) * COEF), 0.0)
            den = den + w * l
            num = num + w * a
        att[rows, :] = mat(back, (num / den).astype(BF)).astype(BF)
        for i in range(2):

            @pl.when(c * 2 + i != h)
            def _():
                hand(c, i).start()

        return carry

    lax.fori_loop(0, NBLK, merge, 0)
    ag[h] = att[pl.ds(pl.multiple_of(h * piece, piece), piece), :]
    pair.wait_recv()
    for copy in relays:
        copy.wait_recv()
    for copy in sends + wcopies + [pair] + relays + qcopies:
        copy.wait_send()
    for j in range(HEADS):

        @pl.when(j != h)
        def _():
            remote(att.at[pl.ds(0, piece)], ag.at[j], asend.at[j], arecv.at[j], (s_idx, j)).wait()

    lhs = jnp.concatenate([ag[i] for i in range(HEADS)], axis=1)
    out_ref[...] = mat(lhs, wf[...].reshape(HEADS * HD, HEADS * HD)).astype(BF)


def on_device(tokens, w_qkv, w_out, offsets):
    hbm = pl.BlockSpec(memory_space=pltpu.HBM)
    dma = pltpu.SemaphoreType.DMA
    vm = pltpu.VMEM
    return pl.pallas_call(
        kernel,
        out_shape=jax.ShapeDtypeStruct((ROWS // HEADS, HEADS * HD), BF),
        in_specs=[hbm] * 4,
        out_specs=pl.BlockSpec(memory_space=pltpu.VMEM),
        scratch_shapes=[
            pltpu.SMEM((NB, HEADS), I32),
            vm((ROWS, HEADS * HD), BF),
            vm((HEADS * HD, 2 * HD), BF),
            vm((HEADS * HD, HD), BF),
            vm((HD, HEADS * HD), BF),
            vm((2, RING, HALF, 2 * HD), BF),
            vm((QTOT + Q1, ROWS), BF),
            vm((QTOT, HALF), BF),
            vm((Q1, ROWS), BF),
            vm((RING, ROWS, 2 * HD), BF),
            *(vm((RING * PICK[b], 2 * HD), BF) for b in range(1, NB)),
            vm((ROWS, HD), BF),
            vm((QTOT + Q1, HD), BF),
            vm((LINES, QTOT, HD), BF),
            vm((LINES, QTOT, 2 * HD), BF),
            vm((LINES, QTOT, 2 * HD), BF),
            vm((ROWS, HD), BF),
            vm((HEADS, ROWS // HEADS, HD), BF),
            vm((HEADS, HD, HEADS * HD), BF),
            vm((ROWS, HD), F32),
            vm((2, ROWS, HD), F32),
            *(vm((3, PICK[b], HD), F32) for b in range(1, NB)),
            dma((8,)),
            dma((2, 2, 4, CHUNKS)),
            dma((2, 2, 4, CHUNKS)),
            *[dma((LINES,))] * 4,
            *[dma((7,))] * 2,
            *[dma((HEADS,))] * 2,
        ],
        compiler_params=pltpu.CompilerParams(
            collective_id=0, has_side_effects=True, vmem_limit_bytes=50 * 1024 * 1024
        ),
    )(offsets, tokens, w_qkv, w_out)


def solution(mesh):
    in_specs = (P("seq", None), P(None, "head"), P("head", None), P())
    out_specs = P(("seq", "head"), None)
    return jax.shard_map(
        on_device, mesh=mesh, in_specs=in_specs, out_specs=out_specs, check_vma=False
    )
```

time: 57 us -> 55.8 us (0.979)
  Pallas kernels: 52.1 us -> 50.9 us
    pallas_call x1, Pallas kernels: 52.1 us -> 50.9 us  [on_device(): pl.pallas_call(kernel, out_shape=jax.ShapeDtypeStruct((ROWS // HEADS, HEA...]
where the time goes in v2:
time: 55.8 us; the launch traced here: 55.5 us
  Pallas kernels  50.9 us (91%)
  local copies, waits for them, and re-layouts  4.65 us (8%)
    pallas_call x1, Pallas kernels, on_device(): pl.pallas_call(kernel, out_shape=jax.ShapeDtypeStruct((ROWS // HEADS, HEA...  50.9 us
    unnamed x9, local copies, waits for them, and re-layouts  4.65 us

profile of v2, /device:TPU:1, one launch (start us, length us, event | category | flops | bytes accessed | tf_op | source)
XLA Modules:
  0.0 55.5 jit_solution(8486698412912996950)
XLA Ops:
  0.0 0.0 copy-start
  0.0 1.2 %copy-done = bf16[512,1024]{1,0:T(8,128)(2,1)S(1)} copy-done((bf16[512,1024]{1,0:T(8,128)(2,1)S(1)}, bf16[512,1024]{1,0:T(8,128)(2,1)}, u32[]{:S(2)}) %copy-start) | copy-done | bytes 1048600
  1.2 0.0 copy-start.1
  1.2 1.1 %copy-done.1 = bf16[1024,384]{1,0:T(8,128)(2,1)S(1)} copy-done((bf16[1024,384]{1,0:T(8,128)(2,1)S(1)}, bf16[1024,384]{1,0:T(8,128)(2,1)}, u32[]{:S(2)}) %copy-start.1) | copy-done | bytes 786456
  2.4 0.0 copy-start.2
  2.4 0.9 %copy-done.2 = bf16[128,1024]{1,0:T(8,128)(2,1)S(1)} copy-done((bf16[128,1024]{1,0:T(8,128)(2,1)S(1)}, bf16[128,1024]{1,0:T(8,128)(2,1)}, u32[]{:S(2)}) %copy-start.2) | copy-done | bytes 262168
  3.3 0.0 copy-start.3
  3.3 0.7 %copy-done.3 = s32[5,8]{1,0:T(8,128)S(1)} copy-done((s32[5,8]{1,0:T(8,128)S(1)}, s32[5,8]{1,0:T(8,128)}, u32[]{:S(2)}) %copy-start.3) | copy-done | bytes 184
  4.0 50.9 %shard_map.46 = bf16[64,1024]{1,0:T(8,128)(2,1)S(1)} custom-call(s32[5,8]{1,0:T(8,128)S(1)} %copy-done.3, bf16[512,1024]{1,0:T(8,128)(2,1)S(1)} %copy-done, bf16[1024,384]{1,0:T(8,128)(2,1)S(1)} %copy-done.1, bf16[128,1024]{1,0:T(8,128)(2,1)S(1)} %copy-done.2), custom_call_target="tpu_custom_call" | custom-call | tf_op jit(solution)/shard_map/pallas_call | solution.py:434
  54.9 0.7 %copy.6 = bf16[64,1024]{1,0:T(8,128)(2,1)} copy(bf16[64,1024]{1,0:T(8,128)(2,1)S(1)} %shard_map.46) | data formatting | bytes 262144
Async XLA Ops:
  0.0 1.2 %copy-start = (bf16[512,1024]{1,0:T(8,128)(2,1)S(1)}, bf16[512,1024]{1,0:T(8,128)(2,1)}, u32[]{:S(2)}) copy-start(bf16[512,1024]{1,0:T(8,128)(2,1)} %tok_hbm.1) | copy-start | bytes 3145732
  1.2 1.1 %copy-start.1 = (bf16[1024,384]{1,0:T(8,128)(2,1)S(1)}, bf16[1024,384]{1,0:T(8,128)(2,1)}, u32[]{:S(2)}) copy-start(bf16[1024,384]{1,0:T(8,128)(2,1)} %wqkv_hbm.1) | copy-start | bytes 2359300
  2.4 0.9 %copy-start.2 = (bf16[128,1024]{1,0:T(8,128)(2,1)S(1)}, bf16[128,1024]{1,0:T(8,128)(2,1)}, u32[]{:S(2)}) copy-start(bf16[128,1024]{1,0:T(8,128)(2,1)} %wout_hbm.1) | copy-start | bytes 786436
  3.3 0.7 %copy-start.3 = (s32[5,8]{1,0:T(8,128)S(1)}, s32[5,8]{1,0:T(8,128)}, u32[]{:S(2)}) copy-start(s32[5,8]{1,0:T(8,128)} %off_hbm.1) | copy-start | bytes 484

commit v3 on v2

--- a/solution.py
+++ b/solution.py
@@ -17,7 +17,7 @@
 BLK = 128
 NBLK = ROWS // BLK
 HALF = ROWS // 2
-CHUNKS = NBLK
+CHUNKS = 4
 CH = HALF // CHUNKS
 PICK = [ROWS >> b for b in range(NB)]
 PER = [BLK >> b for b in range(NB)]
@@ -31,8 +31,21 @@
 I32 = jnp.int32
 
 
+STATS = 16
+PBASE = {4: 0, 3: Q4 + STATS, 2: Q4 + Q3 + 2 * STATS}
+PTOT = QTOT + 3 * STATS
+
+
 def prefix(j):
     return QTOT if j == 1 else (Q4 + Q3 if j < 4 else Q4)
+
+
+def prefix_part(j):
+    return PTOT if j == 1 else (PBASE[2] if j < 4 else PBASE[3])
+
+
+QALL = sum(prefix(j) for j in range(1, LINES))
+PALL = sum(prefix_part(j) for j in range(1, LINES))
 
 
 def xor(a, j):
@@ -95,9 +108,13 @@
     return out.astype(BF)
 
 
-def unpack(block):
-    a = block[:, :HD].astype(F32)
-    t = block[:, HD:].astype(F32)
+def turn(a, b):
+    return lax.dot_general(a, b, (((1,), (1,)), ((), ())), preferred_element_type=F32)
+
+
+def unpack(block, n):
+    a = block[:n].astype(F32)
+    t = turn(onehot(iota((n, 1), 0), iota((1, n), 1)), block[n : n + STATS, :n])
     m = t[:, 0:1] + (t[:, 1:2] + t[:, 2:3])
     l = t[:, 3:4] + (t[:, 4:5] + t[:, 5:6])
     return m, l, a
@@ -106,8 +123,8 @@
 def kernel(
     off_hbm, tok_hbm, wqkv_hbm, wout_hbm, out_ref,
     off, tok, wkv, wq, wout, rings, selq, sela, selb, kb0, kb1, kb2, kb3, kb4, qb, qs, rq, ps, ro,
-    att, ag, wf, acc0, st0, res1, res2, res3, res4,
-    insem, ysend, yrecv, qsend, qrecv, psend, precv, wsend, wrecv, asend, arecv,
+    att, ag, wf, spare, acc0, st0, res1, res2, res3, res4,
+    insem, ysend, yrecv, zsend, zrecv, wsend, wrecv, asem,
 ):
     s_idx = lax.axis_index("seq")
     h = lax.axis_index("head")
@@ -117,7 +134,7 @@
     loads = [
         (off_hbm, off),
         (wqkv_hbm.at[:, pl.ds(HD, 2 * HD)], wkv),
-        *((tok_hbm.at[pl.ds(c * BLK, BLK)], tok.at[pl.ds(c * BLK, BLK)]) for c in range(NBLK)),
+        *((tok_hbm.at[pl.ds(c * BLK, BLK)], tok.at[pl.ds(c * BLK, BLK)]) for c in range(4)),
         (wqkv_hbm.at[:, pl.ds(0, HD)], wq),
         (wout_hbm, wout),
     ]
@@ -164,6 +181,47 @@
     for rho in range(RES):
         rank = jnp.where((lane & 15) == rho, ranks[rho], rank)
     travel = onehot(iota((BLK, 1), 0), rank * 8 + (lane >> 4))
+
+    own, sides, far = 0, [[1, 3, 5], [2, 4, 6]], 7
+    flow_peer = [(at_y(-1), h), (at_y(1), h)]
+
+    def ring(ph, d, hop, c):
+        slots = [own] + sides[d] + [far]
+        rows = pl.ds(c * CH, CH)
+        recv = yrecv.at[(ph * 2 + d) * 14 + (hop * CHUNKS + c if hop < 3 else 12 + c % 2)]
+        return remote(
+            rings.at[ph, slots[hop], rows], rings.at[ph, slots[hop + 1], rows],
+            ysend.at[0], recv, flow_peer[d],
+        )
+
+    def last(d):
+        return range(CHUNKS // 2) if d == 0 else range(CHUNKS // 2, CHUNKS)
+
+    def send(ph, hop, c):
+        for d in range(2):
+            ring(ph, d, hop, c).start()
+
+    def arrive(ph, hop):
+        for c in range(CHUNKS):
+            for d in range(2):
+                if hop < 3 or c in last(d):
+                    ring(ph, d, hop, c).wait_recv()
+                    if hop < 2 or (hop == 2 and c in last(d)):
+                        ring(ph, d, hop + 1, c).start()
+
+    loads[1].wait()
+    for c in range(CHUNKS):
+        loads[2 + c].wait()
+        kv = mat(tok[c * BLK : (c + 1) * BLK], wkv[...]).astype(BF)
+        for i in range(1):
+            part = mat(travel, kv[i * BLK : (i + 1) * BLK]).astype(BF)
+            at = c * CH + i * (BLK // 2)
+            rings[0, own, at : at + BLK // 2] = part[: BLK // 2]
+            rings[1, own, at : at + BLK // 2] = part[BLK // 2 :]
+        if c == 0:
+            pl.semaphore_wait(barrier, len(peers))
+        send(0, 0, c)
+
     place = iota((1, ROWS), 1)
     group = ((place >> 3) & 7) + ((place >> 8) << 3)
     label = jnp.zeros((1, ROWS), I32)
@@ -181,50 +239,6 @@
     static = onehot(home(iota((BLK, 1), 0)), iota((1, BLK), 1))
     back = onehot(iota((BLK, 1), 0), home(iota((1, BLK), 1)))
 
-    own, sides, far = 0, [[1, 3, 5], [2, 4, 6]], 7
-    flow_peer = [(at_y(-1), h), (at_y(1), h)]
-
-    def ring(ph, d, hop, c):
-        slots = [own] + sides[d] + [far]
-        rows = pl.ds(c * CH, CH)
-        return remote(
-            rings.at[ph, slots[hop], rows], rings.at[ph, slots[hop + 1], rows],
-            ysend.at[ph, d, hop, c], yrecv.at[ph, d, hop, c], flow_peer[d],
-        )
-
-    def last(d):
-        return range(CHUNKS // 2) if d == 0 else range(CHUNKS // 2, CHUNKS)
-
-    sends = []
-
-    def send(ph, hop, c):
-        for d in range(2):
-            if hop < 3 or c in last(d):
-                copy = ring(ph, d, hop, c)
-                copy.start()
-                sends.append(copy)
-
-    def arrive(ph, hop):
-        for c in range(CHUNKS):
-            for d in range(2):
-                if hop < 3 or c in last(d):
-                    ring(ph, d, hop, c).wait_recv()
-                    if hop < 2 or (hop == 2 and c in last(d)):
-                        copy = ring(ph, d, hop + 1, c)
-                        copy.start()
-                        sends.append(copy)
-
-    loads[1].wait()
-    for c in range(NBLK):
-        loads[2 + c].wait()
-        kv = mat(tok[c * BLK : (c + 1) * BLK], wkv[...]).astype(BF)
-        kv = mat(travel, kv).astype(BF)
-        rings[0, own, c * CH : (c + 1) * CH] = kv[:CH]
-        rings[1, own, c * CH : (c + 1) * CH] = kv[CH:]
-        if c == 0:
-            pl.semaphore_wait(barrier, len(peers))
-        send(0, 0, c)
-
     loads[6].wait()
     for c in range(NBLK):
         rows = slice(c * BLK, (c + 1) * BLK)
@@ -236,28 +250,25 @@
         key = (row >> shift) * BLK + revs[b] * per + (row & (per - 1))
         selq[BASE[b] : BASE[b] + n] = onehot(key, place)
     qs[...] = mat(selq[...], qb[...]).astype(BF)
-    qcopies = []
     for j in range(1, LINES):
         n = prefix(j)
-        copy = remote(
-            qs.at[pl.ds(0, n)], rq.at[j, pl.ds(0, n)], qsend.at[j], qrecv.at[j],
+        remote(
+            qs.at[pl.ds(0, n)], rq.at[j, pl.ds(0, n)], zsend.at[0], zrecv.at[0],
             (xor(z, j) * RING + y, h),
-        )
-        copy.start()
-        qcopies.append(copy)
+        ).start()
+    qall = remote(spare.at[pl.ds(0, QALL)], spare.at[pl.ds(0, QALL)], zsend.at[0], zrecv.at[0], peers[2])
+    pall = remote(spare, spare, zsend.at[1], zrecv.at[1], peers[2])
 
     loads[7].wait()
-    wcopies = []
     for dx in range(1, 4):
-        copy = remote(
-            wout, wf.at[h], wsend.at[dx], wrecv.at[dx], (s_idx, lax.rem(x + dx, 4) * 2 + core)
-        )
-        copy.start()
-        wcopies.append(copy)
+        to = (s_idx, lax.rem(x + dx, 4) * 2 + core)
+        remote(wout, wf.at[h], wsend.at[0], wrecv.at[0], to).start()
     sibling = (s_idx, x * 2 + 1 - core)
-    pair = remote(wout, wf.at[h], wsend.at[0], wrecv.at[0], sibling)
-    pair.start()
+    remote(wout, wf.at[h], wsend.at[0], wrecv.at[1], sibling).start()
     wf[h] = wout[...]
+
+    def wall(n, sem):
+        return remote(wf.at[pl.ds(0, n)], wf.at[pl.ds(0, n)], wsend.at[0], sem, sibling)
 
     signed = [0, 1, -1, 2, -2, 3, -3, 4]
 
@@ -287,8 +298,7 @@
         send(1, 0, c)
     take_a(5)
     take_a(6)
-    for copy in qcopies:
-        copy.wait_recv()
+    qall.wait_recv()
     q1 = qs[QTOT : QTOT + Q1]
     q2 = jnp.concatenate([qs[Q4 + Q3 : QTOT], rq[1, Q4 + Q3 : QTOT]], axis=0)
     q3 = jnp.concatenate([qs[Q4 : Q4 + Q3]] + [rq[j, Q4 : Q4 + Q3] for j in range(1, 4)], axis=0)
@@ -296,22 +306,23 @@
     arrive(0, 3)
     take_a(far)
 
+    pick = onehot(iota((STATS, 1), 0), iota((1, HD), 1))
     mine = {}
     for b, qq, kb in ((4, q4, kb4), (3, q3, kb3), (2, q2, kb2)):
         m, l, a = attend(qq, kb[...])
-        n, base, lines = PICK[b], BASE[b], 1 << (b - 1)
+        n, base, lines = PICK[b], PBASE[b], 1 << (b - 1)
         mine[b] = (m[:n], l[:n], a[:n])
-        msg = jnp.concatenate([a.astype(BF), pack(m, l)], axis=1)
+        stats = pack(m, l)
         for j in range(1, lines):
-            ps[j, base : base + n] = msg[j * n : (j + 1) * n]
+            part = slice(j * n, (j + 1) * n)
+            ps[j, base : base + n] = a[part].astype(BF)
+            ps[j, base + n : base + n + STATS, :n] = turn(pick, stats[part]).astype(BF)
         for j in range(lines // 2, lines):
-            k = prefix(j)
-            copy = remote(
-                ps.at[j, pl.ds(0, k)], ro.at[j, pl.ds(0, k)], psend.at[j], precv.at[j],
+            k = prefix_part(j)
+            remote(
+                ps.at[j, pl.ds(0, k)], ro.at[j, pl.ds(0, k)], zsend.at[1], zrecv.at[1],
                 (xor(z, j) * RING + y, h),
-            )
-            copy.start()
-            qcopies.append(copy)
+            ).start()
 
     def keep(res, part):
         m, l, a = part
@@ -323,13 +334,10 @@
     arrive(1, 0)
     take_b(1)
     take_b(2)
-    relays = []
+    wall(3, wrecv.at[0]).wait_recv()
     for dx in range(1, 4):
-        wcopies[dx - 1].wait_recv()
         slot = lax.rem(x + 4 - dx, 4) * 2 + core
-        copy = remote(wf.at[slot], wf.at[slot], wsend.at[3 + dx], wrecv.at[3 + dx], sibling)
-        copy.start()
-        relays.append(copy)
+        remote(wf.at[slot], wf.at[slot], wsend.at[0], wrecv.at[1], sibling).start()
     arrive(1, 1)
     take_b(3)
     take_b(4)
@@ -362,11 +370,10 @@
     take_b(6)
     lax.fori_loop(0, 2, tile2, 0)
     second = attend(q1, kb1[5 * Q1 : 7 * Q1])
-    for copy in qcopies[LINES - 1 :]:
-        copy.wait_recv()
+    pall.wait_recv()
     for b, res in ((2, res2), (3, res3), (4, res4)):
-        n, base = PICK[b], BASE[b]
-        parts = [unpack(ro[j, base : base + n]) for j in range(1, 1 << (b - 1))]
+        n, base = PICK[b], PBASE[b]
+        parts = [unpack(ro[j, base : base + n + STATS], n) for j in range(1, 1 << (b - 1))]
         keep(res, join([mine[b]] + parts))
     arrive(1, 3)
     take_b(far)
@@ -377,7 +384,7 @@
     def hand(c, i):
         to = c * 2 + i
         rows = pl.ds(pl.multiple_of(to * piece, piece), piece)
-        return remote(att.at[rows], ag.at[h], asend.at[to], arecv.at[h], (s_idx, to))
+        return remote(att.at[rows], ag.at[h], asem.at[0], asem.at[1], (s_idx, to))
 
     def merge(step, carry):
         t = NBLK - 1 - step
@@ -412,16 +419,13 @@
 
     lax.fori_loop(0, NBLK, merge, 0)
     ag[h] = att[pl.ds(pl.multiple_of(h * piece, piece), piece), :]
-    pair.wait_recv()
-    for copy in relays:
-        copy.wait_recv()
-    for copy in sends + wcopies + [pair] + relays + qcopies:
-        copy.wait_send()
-    for j in range(HEADS):
-
-        @pl.when(j != h)
-        def _():
-            remote(att.at[pl.ds(0, piece)], ag.at[j], asend.at[j], arecv.at[j], (s_idx, j)).wait()
+    wall(4, wrecv.at[1]).wait_recv()
+    wall(7, wrecv.at[1]).wait_send()
+    qall.wait_send()
+    pall.wait_send()
+    moved = rings.at[:, pl.ds(0, 7)]
+    remote(moved, moved, ysend.at[0], yrecv.at[0], flow_peer[0]).wait_send()
+    remote(ag.at[pl.ds(0, 7)], ag.at[pl.ds(0, 7)], asem.at[0], asem.at[1], sibling).wait()
 
     lhs = jnp.concatenate([ag[i] for i in range(HEADS)], axis=1)
     out_ref[...] = mat(lhs, wf[...].reshape(HEADS * HD, HEADS * HD)).astype(BF)
@@ -451,20 +455,23 @@
             vm((ROWS, HD), BF),
             vm((QTOT + Q1, HD), BF),
             vm((LINES, QTOT, HD), BF),
-            vm((LINES, QTOT, 2 * HD), BF),
-            vm((LINES, QTOT, 2 * HD), BF),
+            vm((LINES, PTOT, HD), BF),
+            vm((LINES, PTOT, HD), BF),
             vm((ROWS, HD), BF),
             vm((HEADS, ROWS // HEADS, HD), BF),
             vm((HEADS, HD, HEADS * HD), BF),
+            vm((PALL, HD), BF),
             vm((ROWS, HD), F32),
             vm((2, ROWS, HD), F32),
             *(vm((3, PICK[b], HD), F32) for b in range(1, NB)),
             dma((8,)),
-            dma((2, 2, 4, CHUNKS)),
-            dma((2, 2, 4, CHUNKS)),
-            *[dma((LINES,))] * 4,
-            *[dma((7,))] * 2,
-            *[dma((HEADS,))] * 2,
+            dma((1,)),
+            dma((56,)),
+            dma((2,)),
+            dma((2,)),
+            dma((1,)),
+            dma((2,)),
+            dma((2,)),
         ],
         compiler_params=pltpu.CompilerParams(
             collective_id=0, has_side_effects=True, vmem_limit_bytes=50 * 1024 * 1024

time: 55.8 us -> 54.7 us (0.980)
  Pallas kernels: 50.9 us -> 49.7 us
    pallas_call x1, Pallas kernels: 50.9 us -> 49.7 us  [on_device(): pl.pallas_call(kernel, out_shape=jax.ShapeDtypeStruct((ROWS // HEADS, HEA...]
where the time goes in v3:
time: 54.7 us; the launch traced here: 54.4 us
  Pallas kernels  49.7 us (91%)
  local copies, waits for them, and re-layouts  4.65 us (9%)
    pallas_call x1, Pallas kernels, on_device(): pl.pallas_call(kernel, out_shape=jax.ShapeDtypeStruct((ROWS // HEADS, HEA...  49.7 us
    unnamed x9, local copies, waits for them, and re-layouts  4.65 us

profile of v3, /device:TPU:1, one launch (start us, length us, event | category | flops | bytes accessed | tf_op | source)
XLA Modules:
  0.0 54.4 jit_solution(11867343797956570995)
XLA Ops:
  0.0 0.0 copy-start
  0.0 1.2 %copy-done = bf16[512,1024]{1,0:T(8,128)(2,1)S(1)} copy-done((bf16[512,1024]{1,0:T(8,128)(2,1)S(1)}, bf16[512,1024]{1,0:T(8,128)(2,1)}, u32[]{:S(2)}) %copy-start) | copy-done | bytes 1048600
  1.2 0.0 copy-start.1
  1.2 1.1 %copy-done.1 = bf16[1024,384]{1,0:T(8,128)(2,1)S(1)} copy-done((bf16[1024,384]{1,0:T(8,128)(2,1)S(1)}, bf16[1024,384]{1,0:T(8,128)(2,1)}, u32[]{:S(2)}) %copy-start.1) | copy-done | bytes 786456
  2.4 0.0 copy-start.2
  2.4 0.9 %copy-done.2 = bf16[128,1024]{1,0:T(8,128)(2,1)S(1)} copy-done((bf16[128,1024]{1,0:T(8,128)(2,1)S(1)}, bf16[128,1024]{1,0:T(8,128)(2,1)}, u32[]{:S(2)}) %copy-start.2) | copy-done | bytes 262168
  3.3 0.0 copy-start.3
  3.3 0.7 %copy-done.3 = s32[5,8]{1,0:T(8,128)S(1)} copy-done((s32[5,8]{1,0:T(8,128)S(1)}, s32[5,8]{1,0:T(8,128)}, u32[]{:S(2)}) %copy-start.3) | copy-done | bytes 184
  4.0 49.7 %shard_map.46 = bf16[64,1024]{1,0:T(8,128)(2,1)S(1)} custom-call(s32[5,8]{1,0:T(8,128)S(1)} %copy-done.3, bf16[512,1024]{1,0:T(8,128)(2,1)S(1)} %copy-done, bf16[1024,384]{1,0:T(8,128)(2,1)S(1)} %copy-done.1, bf16[128,1024]{1,0:T(8,128)(2,1)S(1)} %copy-done.2), custom_call_target="tpu_custom_call" | custom-call | tf_op jit(solution)/shard_map/pallas_call | solution.py:438
  53.8 0.7 %copy.6 = bf16[64,1024]{1,0:T(8,128)(2,1)} copy(bf16[64,1024]{1,0:T(8,128)(2,1)S(1)} %shard_map.46) | data formatting | bytes 262144
Async XLA Ops:
  0.0 1.2 %copy-start = (bf16[512,1024]{1,0:T(8,128)(2,1)S(1)}, bf16[512,1024]{1,0:T(8,128)(2,1)}, u32[]{:S(2)}) copy-start(bf16[512,1024]{1,0:T(8,128)(2,1)} %tok_hbm.1) | copy-start | bytes 3145732
  1.2 1.1 %copy-start.1 = (bf16[1024,384]{1,0:T(8,128)(2,1)S(1)}, bf16[1024,384]{1,0:T(8,128)(2,1)}, u32[]{:S(2)}) copy-start(bf16[1024,384]{1,0:T(8,128)(2,1)} %wqkv_hbm.1) | copy-start | bytes 2359300
  2.4 0.9 %copy-start.2 = (bf16[128,1024]{1,0:T(8,128)(2,1)S(1)}, bf16[128,1024]{1,0:T(8,128)(2,1)}, u32[]{:S(2)}) copy-start(bf16[128,1024]{1,0:T(8,128)(2,1)} %wout_hbm.1) | copy-start | bytes 786436
  3.3 0.7 %copy-start.3 = (s32[5,8]{1,0:T(8,128)S(1)}, s32[5,8]{1,0:T(8,128)}, u32[]{:S(2)}) copy-start(s32[5,8]{1,0:T(8,128)} %off_hbm.1) | copy-start | bytes 484

commit v4 on v3

--- a/solution.py
+++ b/solution.py
@@ -201,13 +201,15 @@
         for d in range(2):
             ring(ph, d, hop, c).start()
 
-    def arrive(ph, hop):
+    def arrive(ph, hop, fill=()):
         for c in range(CHUNKS):
             for d in range(2):
                 if hop < 3 or c in last(d):
                     ring(ph, d, hop, c).wait_recv()
                     if hop < 2 or (hop == 2 and c in last(d)):
                         ring(ph, d, hop + 1, c).start()
+            if c < len(fill):
+                fill[c]()
 
     loads[1].wait()
     for c in range(CHUNKS):
@@ -308,7 +310,7 @@
 
     pick = onehot(iota((STATS, 1), 0), iota((1, HD), 1))
     mine = {}
-    for b, qq, kb in ((4, q4, kb4), (3, q3, kb3), (2, q2, kb2)):
+    def line(b, qq, kb):
         m, l, a = attend(qq, kb[...])
         n, base, lines = PICK[b], PBASE[b], 1 << (b - 1)
         mine[b] = (m[:n], l[:n], a[:n])
@@ -330,8 +332,9 @@
         res[1] = jnp.broadcast_to(m, a.shape)
         res[2] = jnp.broadcast_to(l, a.shape)
 
+    lines = [(4, q4, kb4), (3, q3, kb3), (2, q2, kb2)]
+    arrive(1, 0, [lambda args=args: line(*args) for args in lines])
     take_b(0)
-    arrive(1, 0)
     take_b(1)
     take_b(2)
     wall(3, wrecv.at[0]).wait_recv()
@@ -363,9 +366,11 @@
         st0[1, rows, :] = l
         return carry
 
-    lax.fori_loop(0, 2, tile, 0)
-    first = attend(q1, kb1[0 : 5 * Q1])
-    arrive(1, 2)
+    first = []
+    arrive(
+        1, 2,
+        [lambda: tile(0, 0), lambda: tile(1, 0), lambda: first.append(attend(q1, kb1[0 : 5 * Q1]))],
+    )
     take_b(5)
     take_b(6)
     lax.fori_loop(0, 2, tile2, 0)
@@ -375,26 +380,12 @@
         n, base = PICK[b], PBASE[b]
         parts = [unpack(ro[j, base : base + n + STATS], n) for j in range(1, 1 << (b - 1))]
         keep(res, join([mine[b]] + parts))
-    arrive(1, 3)
-    take_b(far)
-    keep(res1, join([first, second, attend(q1, kb1[7 * Q1 : 8 * Q1])]))
-
-    piece = ROWS // HEADS
-
-    def hand(c, i):
-        to = c * 2 + i
-        rows = pl.ds(pl.multiple_of(to * piece, piece), piece)
-        return remote(att.at[rows], ag.at[h], asem.at[0], asem.at[1], (s_idx, to))
-
-    def merge(step, carry):
-        t = NBLK - 1 - step
-        c = lax.rem(x + t + lax.div(t, 2) * (5 - 2 * t), 4)
-        rows = pl.ds(pl.multiple_of(c * BLK, BLK), BLK)
+    def blend(rows, c, group):
         m0, l0, a0 = st0[0, rows, :], st0[1, rows, :], acc0[rows, :]
         place_of = iota((BLK, HD), 0)
         spread = []
         top = m0
-        for b, res in ((1, res1), (2, res2), (3, res3), (4, res4)):
+        for b, res in group:
             per = PER[b]
             part = pl.ds(pl.multiple_of(c * per, per), per)
             a, m, l = (jnp.concatenate([res[i, part, :]] * (1 << b), axis=0) for i in range(3))
@@ -408,6 +399,34 @@
             w = jnp.where(chosen, jnp.exp2((m - top) * COEF), 0.0)
             den = den + w * l
             num = num + w * a
+        return top, den, num
+
+    def premerge(c, carry):
+        rows = pl.ds(pl.multiple_of(c * BLK, BLK), BLK)
+        top, den, num = blend(rows, c, ((1, res1), (2, res2), (3, res3), (4, res4)))
+        st0[0, rows, :] = top
+        st0[1, rows, :] = den
+        acc0[rows, :] = num
+        return carry
+
+    keep(res1, join([first[0], second]))
+    lax.fori_loop(0, NBLK, premerge, 0)
+    arrive(1, 3)
+    take_b(far)
+    keep(res1, attend(q1, kb1[7 * Q1 : 8 * Q1]))
+
+    piece = ROWS // HEADS
+
+    def hand(c, i):
+        to = c * 2 + i
+        rows = pl.ds(pl.multiple_of(to * piece, piece), piece)
+        return remote(att.at[rows], ag.at[h], asem.at[0], asem.at[1], (s_idx, to))
+
+    def merge(step, carry):
+        t = NBLK - 1 - step
+        c = lax.rem(x + t + lax.div(t, 2) * (5 - 2 * t), 4)
+        rows = pl.ds(pl.multiple_of(c * BLK, BLK), BLK)
+        _, den, num = blend(rows, c, ((1, res1),))
         att[rows, :] = mat(back, (num / den).astype(BF)).astype(BF)
         for i in range(2):
 
@@ -476,7 +495,7 @@
         compiler_params=pltpu.CompilerParams(
             collective_id=0, has_side_effects=True, vmem_limit_bytes=50 * 1024 * 1024
         ),
-    )(offsets, tokens, w_qkv, w_out)
+    )(*(pltpu.with_memory_space_constraint(v, pltpu.HBM) for v in (offsets, tokens, w_qkv, w_out)))
 
 
 def solution(mesh):

time: 54.7 us -> 50.7 us (0.927)
  local copies, waits for them, and re-layouts: 4.65 us -> 0.66 us
    unnamed x9 -> x1, local copies, waits for them, and re-layouts: 4.65 us -> 0.66 us
where the time goes in v4:
time: 50.7 us; the launch traced here: 50.6 us
  Pallas kernels  49.9 us (98%)
  local copies, waits for them, and re-layouts  0.66 us (1%)
    pallas_call x1, Pallas kernels, on_device(): pl.pallas_call(kernel, out_shape=jax.ShapeDtypeStruct((ROWS // HEADS, HEA...  49.9 us

profile of v4, /device:TPU:1, one launch (start us, length us, event | category | flops | bytes accessed | tf_op | source)
XLA Modules:
  0.0 50.6 jit_solution(13818890732602671851)
XLA Ops:
  0.0 49.9 %shard_map.46 = bf16[64,1024]{1,0:T(8,128)(2,1)S(1)} custom-call(s32[5,8]{1,0:T(8,128)} %off_hbm.1, bf16[512,1024]{1,0:T(8,128)(2,1)} %tok_hbm.1, bf16[1024,384]{1,0:T(8,128)(2,1)} %wqkv_hbm.1, bf16[128,1024]{1,0:T(8,128)(2,1)} %wout_hbm.1), custom_call_target="tpu_custom_call" | custom-call | tf_op jit(solution)/shard_map/pallas_call | solution.py:457
  49.9 0.7 %copy.6 = bf16[64,1024]{1,0:T(8,128)(2,1)} copy(bf16[64,1024]{1,0:T(8,128)(2,1)S(1)} %shard_map.46) | data formatting | bytes 262144

commit v5 on v4

--- a/solution.py
+++ b/solution.py
@@ -261,6 +261,28 @@
     qall = remote(spare.at[pl.ds(0, QALL)], spare.at[pl.ds(0, QALL)], zsend.at[0], zrecv.at[0], peers[2])
     pall = remote(spare, spare, zsend.at[1], zrecv.at[1], peers[2])
 
+    signed = [0, 1, -1, 2, -2, 3, -3, 4]
+
+    def take_a(slot):
+        block = rings[0, slot]
+        if slot != far:
+            kb0[lax.rem(y + RING + signed[slot], RING), 0:HALF] = block
+        taken = mat(sela[...], block).astype(BF)
+        for b, buf in ((2, kb2), (3, kb3), (4, kb4)):
+            n = PICK[b]
+            buf[slot * n : (slot + 1) * n] = taken[BASE[b] : BASE[b] + n]
+
+    def take_b(slot):
+        block = rings[1, slot]
+        if slot != far:
+            kb0[lax.rem(y + RING + signed[slot], RING), HALF:ROWS] = block
+        both = mat(selb[:, :HALF], rings[0, slot]) + mat(selb[:, HALF:], block)
+        if slot == far:
+            return both.astype(BF)
+        kb1[slot * Q1 : (slot + 1) * Q1] = both.astype(BF)
+
+    arrive(0, 0)
+
     loads[7].wait()
     for dx in range(1, 4):
         to = (s_idx, lax.rem(x + dx, 4) * 2 + core)
@@ -272,24 +294,7 @@
     def wall(n, sem):
         return remote(wf.at[pl.ds(0, n)], wf.at[pl.ds(0, n)], wsend.at[0], sem, sibling)
 
-    signed = [0, 1, -1, 2, -2, 3, -3, 4]
-
-    def take_a(slot):
-        block = rings[0, slot]
-        kb0[lax.rem(y + RING + signed[slot], RING), 0:HALF] = block
-        taken = mat(sela[...], block).astype(BF)
-        for b, buf in ((2, kb2), (3, kb3), (4, kb4)):
-            n = PICK[b]
-            buf[slot * n : (slot + 1) * n] = taken[BASE[b] : BASE[b] + n]
-
-    def take_b(slot):
-        block = rings[1, slot]
-        kb0[lax.rem(y + RING + signed[slot], RING), HALF:ROWS] = block
-        both = mat(selb[:, :HALF], rings[0, slot]) + mat(selb[:, HALF:], block)
-        kb1[slot * Q1 : (slot + 1) * Q1] = both.astype(BF)
-
     take_a(0)
-    arrive(0, 0)
     take_a(1)
     take_a(2)
     arrive(0, 1)
@@ -412,31 +417,23 @@
     keep(res1, join([first[0], second]))
     lax.fori_loop(0, NBLK, premerge, 0)
     arrive(1, 3)
-    take_b(far)
-    keep(res1, attend(q1, kb1[7 * Q1 : 8 * Q1]))
+    keep(res1, attend(q1, take_b(far)))
 
     piece = ROWS // HEADS
 
-    def hand(c, i):
-        to = c * 2 + i
+    def hand(to, dx):
         rows = pl.ds(pl.multiple_of(to * piece, piece), piece)
-        return remote(att.at[rows], ag.at[h], asem.at[0], asem.at[1], (s_idx, to))
-
-    def merge(step, carry):
-        t = NBLK - 1 - step
-        c = lax.rem(x + t + lax.div(t, 2) * (5 - 2 * t), 4)
+        remote(att.at[rows], ag.at[h], asem.at[0], asem.at[1 + dx], (s_idx, to)).start()
+
+    for dx in (2, 1, 3, 0):
+        c = lax.rem(x + dx, 4)
         rows = pl.ds(pl.multiple_of(c * BLK, BLK), BLK)
         _, den, num = blend(rows, c, ((1, res1),))
         att[rows, :] = mat(back, (num / den).astype(BF)).astype(BF)
-        for i in range(2):
-
-            @pl.when(c * 2 + i != h)
-            def _():
-                hand(c, i).start()
-
-        return carry
-
-    lax.fori_loop(0, NBLK, merge, 0)
+        if dx:
+            hand(c * 2 + core, dx)
+        hand(c * 2 + 1 - core, dx)
+
     ag[h] = att[pl.ds(pl.multiple_of(h * piece, piece), piece), :]
     wall(4, wrecv.at[1]).wait_recv()
     wall(7, wrecv.at[1]).wait_send()
@@ -444,10 +441,19 @@
     pall.wait_send()
     moved = rings.at[:, pl.ds(0, 7)]
     remote(moved, moved, ysend.at[0], yrecv.at[0], flow_peer[0]).wait_send()
-    remote(ag.at[pl.ds(0, 7)], ag.at[pl.ds(0, 7)], asem.at[0], asem.at[1], sibling).wait()
-
-    lhs = jnp.concatenate([ag[i] for i in range(HEADS)], axis=1)
-    out_ref[...] = mat(lhs, wf[...].reshape(HEADS * HD, HEADS * HD)).astype(BF)
+    def product(dx):
+        block = ag.at[pl.ds(0, 2 if dx else 1)]
+        remote(block, block, asem.at[0], asem.at[1 + dx], sibling).wait_recv()
+        pair = pl.ds(lax.rem(x + 4 - dx, 4) * 2, 2)
+        lhs = ag[pair]
+        lhs = jnp.concatenate([lhs[0], lhs[1]], axis=1)
+        return mat(lhs, wf[pair].reshape(2 * HD, HEADS * HD))
+
+    mixed = product(0)
+    for dx in (1, 3, 2):
+        mixed = mixed + product(dx)
+    out_ref[...] = mixed.astype(BF)
+    remote(ag.at[pl.ds(0, 7)], ag.at[pl.ds(0, 7)], asem.at[0], asem.at[1], sibling).wait_send()
 
 
 def on_device(tokens, w_qkv, w_out, offsets):
@@ -470,7 +476,8 @@
             vm((QTOT, HALF), BF),
             vm((Q1, ROWS), BF),
             vm((RING, ROWS, 2 * HD), BF),
-            *(vm((RING * PICK[b], 2 * HD), BF) for b in range(1, NB)),
+            vm(((RING - 1) * Q1, 2 * HD), BF),
+            *(vm((RING * PICK[b], 2 * HD), BF) for b in range(2, NB)),
             vm((ROWS, HD), BF),
             vm((QTOT + Q1, HD), BF),
             vm((LINES, QTOT, HD), BF),
@@ -490,7 +497,7 @@
             dma((2,)),
             dma((1,)),
             dma((2,)),
-            dma((2,)),
+            dma((5,)),
         ],
         compiler_params=pltpu.CompilerParams(
             collective_id=0, has_side_effects=True, vmem_limit_bytes=50 * 1024 * 1024

time: 50.7 us -> 50.5 us (level)
  no operation moved by 1% of the time
where the time goes in v5:
time: 50.5 us; the launch traced here: 50.3 us
  Pallas kernels  49.7 us (98%)
  local copies, waits for them, and re-layouts  0.66 us (1%)
    pallas_call x1, Pallas kernels, on_device(): pl.pallas_call(kernel, out_shape=jax.ShapeDtypeStruct((ROWS // HEADS, HEA...  49.7 us

profile of v5, /device:TPU:1, one launch (start us, length us, event | category | flops | bytes accessed | tf_op | source)
XLA Modules:
  0.0 50.3 jit_solution(11757593408624549291)
XLA Ops:
  0.0 49.7 %shard_map.46 = bf16[64,1024]{1,0:T(8,128)(2,1)S(1)} custom-call(s32[5,8]{1,0:T(8,128)} %off_hbm.1, bf16[512,1024]{1,0:T(8,128)(2,1)} %tok_hbm.1, bf16[1024,384]{1,0:T(8,128)(2,1)} %wqkv_hbm.1, bf16[128,1024]{1,0:T(8,128)(2,1)} %wout_hbm.1), custom_call_target="tpu_custom_call" | custom-call | tf_op jit(solution)/shard_map/pallas_call | solution.py:463
  49.7 0.7 %copy.6 = bf16[64,1024]{1,0:T(8,128)(2,1)} copy(bf16[64,1024]{1,0:T(8,128)(2,1)S(1)} %shard_map.46) | data formatting | bytes 262144

commit v6 on v5

--- a/solution.py
+++ b/solution.py
@@ -298,11 +298,11 @@
     take_a(1)
     take_a(2)
     arrive(0, 1)
+    for c in range(CHUNKS):
+        send(1, 0, c)
     take_a(3)
     take_a(4)
     arrive(0, 2)
-    for c in range(CHUNKS):
-        send(1, 0, c)
     take_a(5)
     take_a(6)
     qall.wait_recv()

time: 50.5 us -> 50 us (0.990)
  no operation moved by 1% of the time
where the time goes in v6:
time: 50 us; the launch traced here: 49.9 us
  Pallas kernels  49.2 us (98%)
  local copies, waits for them, and re-layouts  0.66 us (1%)
    pallas_call x1, Pallas kernels, on_device(): pl.pallas_call(kernel, out_shape=jax.ShapeDtypeStruct((ROWS // HEADS, HEA...  49.2 us

profile of v6, /device:TPU:1, one launch (start us, length us, event | category | flops | bytes accessed | tf_op | source)
XLA Modules:
  0.0 49.9 jit_solution(8952258513432626433)
XLA Ops:
  0.0 49.2 %shard_map.46 = bf16[64,1024]{1,0:T(8,128)(2,1)S(1)} custom-call(s32[5,8]{1,0:T(8,128)} %off_hbm.1, bf16[512,1024]{1,0:T(8,128)(2,1)} %tok_hbm.1, bf16[1024,384]{1,0:T(8,128)(2,1)} %wqkv_hbm.1, bf16[128,1024]{1,0:T(8,128)(2,1)} %wout_hbm.1), custom_call_target="tpu_custom_call" | custom-call | tf_op jit(solution)/shard_map/pallas_call | solution.py:463
  49.2 0.7 %copy.6 = bf16[64,1024]{1,0:T(8,128)(2,1)} copy(bf16[64,1024]{1,0:T(8,128)(2,1)S(1)} %shard_map.46) | data formatting | bytes 262144
